TPU v7x, 128 devices: a whole 4x4x4 slice. The times are simulated.
128 devices in a mesh: ctx: 16 (over x, y), head: 2 (over core), dp: 4 (over z).
Axes of the slice: x: 4, y: 4, z: 4, core: 2. Of those that a mesh axis runs over, the one named last changes fastest.
Arguments:
- query_matrix: bfloat16 [16384, 4096], P(('dp', 'ctx'), 'head'), parts along dimension 0
- key_matrix: bfloat16 [16384, 512], P(('dp', 'ctx'), 'head'), parts along dimension 0
- value_matrix: bfloat16 [16384, 512], P(('dp', 'ctx'), 'head'), parts along dimension 0, may hold values from -6 to 6
- output_cotangent: bfloat16 [16384, 4096], P(('dp', 'ctx'), 'head'), parts along dimension 0, may hold values from -6 to 6
- doc_lengths: int32 [32], P('dp'), parts along dimension 0, may hold values from 1 to 2304, 4096 in all
- block_dest: int32 [1024], P('dp'), parts along dimension 0, may hold values from 0 to 255, as said below
Outputs:
- attention_result: bfloat16 [16384, 4096], P(('dp', 'ctx'), 'head'), parts along dimension 0
- query_gradient: bfloat16 [16384, 4096], P(('dp', 'ctx'), 'head'), parts along dimension 0
- key_gradient: bfloat16 [16384, 512], P(('dp', 'ctx'), 'head'), parts along dimension 0
- value_gradient: bfloat16 [16384, 512], P(('dp', 'ctx'), 'head'), parts along dimension 0
There are 4 independent parts, one for each index of `dp`. A program takes and returns all parts, laid end to end along the dimension named above; each array names one. Nothing has to cross between parts.
Inputs may be any that keep to these rules, and one draw needn't show every extreme that they name: `doc_lengths`: the 8 lengths sum to 4096. `block_dest`: a permutation; the 16 blocks that start on one index of ctx go at most 2 to one index of ctx (slot k lies on index k // 16), and exactly 2 for some pair of indices.
All inputs are finite; a program needn't handle non-finite values.
Results may differ from a plain program's by a relative error of at most 0.03.
Values may be sent and summed in bfloat16 or wider, within the bound.
A program may use at most 128 MiB of HBM per device.

v0:
```python
import math

import jax
import jax.numpy as jnp
from jax import lax
from jax.sharding import PartitionSpec as P

HEAD_SIZE = 128
BLK = 16


def doc_starts(doc_lengths, positions):
    doc_ends = jnp.cumsum(doc_lengths)
    chosen = jnp.where(doc_ends[None, :] <= positions[:, None], doc_lengths[None, :], 0)
    return jnp.sum(chosen, axis=1)


def shards(query_matrix, key_matrix, value_matrix, output_cotangent, doc_lengths, block_dest):
    devices = lax.axis_size("ctx")
    own_index = lax.axis_index("ctx")
    tok_rows = query_matrix.shape[0]
    blocks_dev = tok_rows // BLK
    kv_heads = key_matrix.shape[1] // HEAD_SIZE
    q_heads = query_matrix.shape[1] // HEAD_SIZE
    head_group = q_heads // kv_heads
    key_width = kv_heads * HEAD_SIZE
    scaling = 1.0 / math.sqrt(HEAD_SIZE)
    capacity = max(2, 2 * blocks_dev // devices)
    all_blocks = devices * blocks_dev
    tile_rows = min(256, tok_rows)
    tiles = tok_rows // tile_rows
    target_dev = (block_dest // blocks_dev).reshape(devices, blocks_dev)
    same_target = target_dev[:, :, None] == target_dev[:, None, :]
    earlier = jnp.arange(blocks_dev)[None, :] < jnp.arange(blocks_dev)[:, None]
    rank_all = jnp.sum(same_target & earlier[None, :, :], axis=-1)
    slot_ids = jnp.arange(all_blocks, dtype=jnp.int32)
    inverse = jnp.sum(
        jnp.where(block_dest[None, :] == slot_ids[:, None], slot_ids[None, :], 0), axis=1
    )
    own_blocks = lax.dynamic_slice_in_dim(inverse, own_index * blocks_dev, blocks_dev)
    work_query, work_grad = (query_matrix, output_cotangent)
    block_ids = own_index * blocks_dev + jnp.arange(blocks_dev, dtype=jnp.int32)
    query_pos = (block_ids[:, None] * BLK + jnp.arange(BLK, dtype=jnp.int32)[None, :]).reshape(
        tiles, tile_rows
    )
    start_pos = doc_starts(doc_lengths, query_pos.reshape(-1)).reshape(tiles, tile_rows)
    query_tiles = work_query.reshape(tiles, tile_rows, kv_heads, head_group, HEAD_SIZE)
    grad_tiles = work_grad.reshape(tiles, tile_rows, kv_heads, head_group, HEAD_SIZE)
    gathered_keys, gathered_values = (
        lax.all_gather(key_matrix, "ctx", axis=0, tiled=True),
        lax.all_gather(value_matrix, "ctx", axis=0, tiled=True),
    )
    key_stack = gathered_keys.reshape(devices, tok_rows, key_width)
    value_stack = gathered_values.reshape(devices, tok_rows, key_width)
    piece_starts = jnp.arange(devices, dtype=jnp.int32) * tok_rows
    key_pieces = key_stack.reshape(-1, tok_rows, kv_heads, HEAD_SIZE)
    value_pieces = value_stack.reshape(-1, tok_rows, kv_heads, HEAD_SIZE)

    def tile_mask(piece_first, tile_pos, tile_start):
        key_pos = piece_first + jnp.arange(tok_rows, dtype=jnp.int32)
        return (key_pos[None, :] >= tile_start[:, None]) & (key_pos[None, :] <= tile_pos[:, None])

    def tile_seen(piece_first, tile_pos, tile_start):
        return jnp.any((piece_first <= tile_pos) & (piece_first + tok_rows - 1 >= tile_start))

    def stats_tile(current, query_tile, tile_pos, tile_start, key_piece, piece_first):
        peak, total = current
        masked = tile_mask(piece_first, tile_pos, tile_start)
        scores = (
            jnp.einsum("rgjd,pgd->gjrp", query_tile, key_piece, preferred_element_type=jnp.float32)
            * scaling
        )
        scores = jnp.where(masked, scores, -1e30)
        new_peak = jnp.maximum(peak, jnp.max(scores, axis=-1))
        weights = jnp.where(masked, jnp.exp(scores - new_peak[..., None]), 0.0)
        total = total * jnp.exp(peak - new_peak) + jnp.sum(weights, axis=-1)
        return (new_peak, total)

    def stats_piece(running, piece):
        key_piece, piece_first = piece
        peaks, totals = running
        query_tile = query_tiles[0]
        tile_pos = query_pos[0]
        tile_start = start_pos[0]
        results = [
            lax.cond(
                tile_seen(piece_first, tile_pos, tile_start),
                lambda current: stats_tile(
                    current, query_tile, tile_pos, tile_start, key_piece, piece_first
                ),
                lambda current: current,
                (peaks[0], totals[0]),
            )
        ]
        peaks = jnp.stack([result[0] for result in results])
        totals = jnp.stack([result[1] for result in results])
        return ((peaks, totals), None)

    initial = (
        jnp.full((tiles, kv_heads, head_group, tile_rows), -1e30, jnp.float32),
        jnp.zeros((tiles, kv_heads, head_group, tile_rows), jnp.float32),
    )
    (peaks, totals), unused_out = lax.scan(stats_piece, initial, (key_pieces, piece_starts))
    lse_tiles = peaks + jnp.log(totals)

    def value_tile(
        accum, query_tile, tile_pos, tile_start, lse_tile, key_piece, value_piece, piece_first
    ):
        masked = tile_mask(piece_first, tile_pos, tile_start)
        scores = (
            jnp.einsum("rgjd,pgd->gjrp", query_tile, key_piece, preferred_element_type=jnp.float32)
            * scaling
        )
        probs_low = jnp.where(masked, jnp.exp(scores - lse_tile[..., None]), 0.0).astype(
            jnp.bfloat16
        )
        return accum + jnp.einsum(
            "gjrp,pgd->gjrd", probs_low, value_piece, preferred_element_type=jnp.float32
        )

    def value_piece_step(accums, piece):
        key_piece, value_piece, piece_first = piece
        query_tile = query_tiles[0]
        tile_pos = query_pos[0]
        tile_start = start_pos[0]
        lse_tile = lse_tiles[0]
        results = [
            lax.cond(
                tile_seen(piece_first, tile_pos, tile_start),
                lambda current: value_tile(
                    current,
                    query_tile,
                    tile_pos,
                    tile_start,
                    lse_tile,
                    key_piece,
                    value_piece,
                    piece_first,
                ),
                lambda current: current,
                accums[0],
            )
        ]
        return (jnp.stack(results), None)

    zero_accum = jnp.zeros((tiles, kv_heads, head_group, tile_rows, HEAD_SIZE), jnp.float32)
    accums, unused_more = lax.scan(
        value_piece_step, zero_accum, (key_pieces, value_pieces, piece_starts)
    )
    attended_tiles = jnp.transpose(accums.astype(jnp.bfloat16), (0, 3, 1, 2, 4))
    delta_tiles = jnp.einsum(
        "trgjd,trgjd->tgjr", grad_tiles, attended_tiles, preferred_element_type=jnp.float32
    )

    def backward_tile(
        current,
        query_tile,
        grad_tile,
        tile_pos,
        tile_start,
        lse_tile,
        delta_tile,
        key_piece,
        value_piece,
        piece_first,
    ):
        grad_key_piece, grad_value_piece, grad_query_tile = current
        masked = tile_mask(piece_first, tile_pos, tile_start)
        scores = (
            jnp.einsum("rgjd,pgd->gjrp", query_tile, key_piece, preferred_element_type=jnp.float32)
            * scaling
        )
        probs = jnp.where(masked, jnp.exp(scores - lse_tile[..., None]), 0.0)
        probs_low = probs.astype(jnp.bfloat16)
        dprobs = jnp.einsum(
            "rgjd,pgd->gjrp", grad_tile, value_piece, preferred_element_type=jnp.float32
        )
        dscores = (probs * (dprobs - delta_tile[..., None])).astype(jnp.bfloat16)
        grad_query_tile = (
            grad_query_tile
            + jnp.einsum("gjrp,pgd->rgjd", dscores, key_piece, preferred_element_type=jnp.float32)
            * scaling
        )
        grad_key_piece = (
            jnp.einsum("gjrp,rgjd->pgd", dscores, query_tile, preferred_element_type=jnp.float32)
            * scaling
        )
        grad_value_piece = jnp.einsum(
            "gjrp,rgjd->pgd", probs_low, grad_tile, preferred_element_type=jnp.float32
        )
        return (grad_key_piece, grad_value_piece, grad_query_tile)

    def backward_piece(grad_query_all, piece):
        key_piece, value_piece, piece_first = piece
        grad_key_piece = jnp.zeros((tok_rows, kv_heads, HEAD_SIZE), jnp.float32)
        grad_value_piece = jnp.zeros((tok_rows, kv_heads, HEAD_SIZE), jnp.float32)
        query_tile = query_tiles[0]
        grad_tile = grad_tiles[0]
        tile_pos = query_pos[0]
        tile_start = start_pos[0]
        lse_tile = lse_tiles[0]
        delta_tile = delta_tiles[0]
        grad_key_piece, grad_value_piece, grad_query_tile = lax.cond(
            tile_seen(piece_first, tile_pos, tile_start),
            lambda current: backward_tile(
                current,
                query_tile,
                grad_tile,
                tile_pos,
                tile_start,
                lse_tile,
                delta_tile,
                key_piece,
                value_piece,
                piece_first,
            ),
            lambda current: current,
            (grad_key_piece, grad_value_piece, grad_query_all[0]),
        )
        grad_query_list = [grad_query_tile]
        return (jnp.stack(grad_query_list), (grad_key_piece, grad_value_piece))

    zero_query = jnp.zeros((tiles, tile_rows, kv_heads, head_group, HEAD_SIZE), jnp.float32)
    grad_query_all, (grad_key_terms, grad_value_terms) = lax.scan(
        backward_piece, zero_query, (key_pieces, value_pieces, piece_starts)
    )
    grad_key_sum, grad_value_sum = (
        lax.psum_scatter(
            grad_key_terms.reshape(devices * tok_rows, key_width),
            "ctx",
            scatter_dimension=0,
            tiled=True,
        ),
        lax.psum_scatter(
            grad_value_terms.reshape(devices * tok_rows, key_width),
            "ctx",
            scatter_dimension=0,
            tiled=True,
        ),
    )
    out_rows = attended_tiles.reshape(tok_rows, q_heads * HEAD_SIZE)
    grad_rows = grad_query_all.astype(jnp.bfloat16).reshape(tok_rows, q_heads * HEAD_SIZE)
    own_target = lax.dynamic_index_in_dim(target_dev, own_index, 0, keepdims=False)
    own_rank = lax.dynamic_index_in_dim(rank_all, own_index, 0, keepdims=False)
    match = (own_target[None, None, :] == jnp.arange(devices)[:, None, None]) & (
        own_rank[None, None, :] == jnp.arange(capacity)[None, :, None]
    )
    source_block = jnp.sum(jnp.where(match, jnp.arange(blocks_dev)[None, None, :], 0), axis=-1)
    filled = jnp.any(match, axis=-1)[:, :, None, None]

    def pack(array):
        picked = array.reshape(blocks_dev, BLK, -1)[source_block]
        return jnp.where(filled, picked, 0).reshape(devices, capacity * BLK, -1)

    got_first = lax.all_to_all(pack(out_rows), "ctx", split_axis=0, concat_axis=0, tiled=True)
    got_second = lax.all_to_all(pack(grad_rows), "ctx", split_axis=0, concat_axis=0, tiled=True)
    anchor_dev = own_blocks // blocks_dev
    anchor_block = own_blocks % blocks_dev
    wanted = anchor_dev * capacity + rank_all[anchor_dev, anchor_block]

    def unpack(got):
        return got.reshape(devices * capacity, BLK, -1)[wanted].reshape(tok_rows, -1)

    final_out = unpack(got_first)
    final_grad = unpack(got_second)
    return (
        final_out,
        final_grad,
        grad_key_sum.astype(jnp.bfloat16),
        grad_value_sum.astype(jnp.bfloat16),
    )


def solution(mesh):
    in_specs = (
        P(("dp", "ctx"), "head"),
        P(("dp", "ctx"), "head"),
        P(("dp", "ctx"), "head"),
        P(("dp", "ctx"), "head"),
        P("dp"),
        P("dp"),
    )
    out_specs = (
        P(("dp", "ctx"), "head"),
        P(("dp", "ctx"), "head"),
        P(("dp", "ctx"), "head"),
        P(("dp", "ctx"), "head"),
    )
    return jax.shard_map(shards, mesh=mesh, in_specs=in_specs, out_specs=out_specs, check_vma=False)
```

profile of v0, /device:TPU:66, one launch (start us, length us, event | category | flops | bytes accessed | tf_op | source)
XLA Modules:
  0.0 752.3 jit_solution(474802347122706081)
XLA Ops:
  9.7 2.4 copy.91
  12.3 44.0 %all-gather.3.cloned.1.call-done = bf16[4096,256]{1,0:T(8,128)(2,1)} async-done(((bf16[256,256]{1,0:T(8,128)(2,1)}), bf16[4096,256]{1,0:T(8,128)(2,1)}) %all-gather.3.cloned.1.call-update) | async-done | bytes 2097168 | tf_op jit(solution)/shard_map/all_gather | solution.py:50
  56.3 2.5 reshape.305
  61.3 81.9 %while.51 = (s32[]{:T(128)}, f32[1,2,8,256]{3,2,1,0:T(8,128)}, f32[1,2,8,256]{3,2,1,0:T(8,128)S(1)}, s32[16]{0:T(128)S(1)}, s32[256]{0:T(256)S(1)}, /*index=5*/b...) while((s32[]{:T(128)}, f32[1,2,8,256]{3,2,1,0:T(8,128)}, ...), condition=%wide.region_10.11_spmd.clone, body=%wide.region_4.10_spmd.clone.sunk | while | flops 277030656 | bytes 12085103 | solution.py:103
  78.8 6.1 conditional.9
  89.2 6.1 conditional.9
  143.3 2.6 reshape.306
  150.0 65.2 %while.52 = (s32[]{:T(128)}, f32[1,2,8,256,128]{4,3,2,1,0:T(8,128)}, s32[16]{0:T(128)S(1)}, s32[256]{0:T(256)S(1)}, bf16[16,256,2,128]{3,1,2,0:T(8,128)(2,1)}, /...) while((s32[]{:T(128)}, ...), condition=%wide.region_15.16_spmd.clone, body=%wide.region_11.15_spmd.clone.sunk | while | flops 541787904 | bytes 7760231 | solution.py:147
  163.3 6.0 conditional.10
  164.4 4.9 add_bitcast_fusion.1
  172.6 6.0 conditional.10
  173.7 4.9 add_bitcast_fusion.1
  215.2 3.1 bitcast_convert_fusion
  221.5 108.0 %while.53 = (s32[]{:T(128)}, f32[1,256,2,8,128]{4,1,3,2,0:T(8,128)}, f32[16,256,2,128]{3,2,1,0:T(2,128)}, f32[16,256,2,128]{3,2,1,0:T(2,128)}, s32[16]{0:T(128)S...) while((s32[]{:T(128)}, ...), condition=%wide.region_22.23_spmd.clone, body=%wide.region_18.22_spmd.clone.sunk | while | flops 1353975552 | bytes 54652384 | solution.py:224
  238.9 16.5 %conditional.11 = (f32[256,2,8,128]{3,0,2,1:T(8,128)}, f32[1,256,2,128]{3,1,2,0:T(8,128)S(1)}, f32[1,256,2,128]{3,1,2,0:T(8,128)S(1)}) conditional(s32[]{:T(128)} %convert_element_type.86, f32[256,2,8,128]{3,0,2,1:T(8,128)} %bitcast.186, (s32[]{:T(128)}, s32[256]{0:T(256)S(1)}, s32[16,16]{1,0:T(8,128)S(1)}, bf16[16,256,2,128]{3,1,2,0:T(8,128)(2,1)}, ...), branch_computations={%region_20.20_spmd, %region_21.21_spmd} | conditional | flops 1353974016 | bytes 53599828 | solution.py:203
  239.2 3.6 fusion.44
  244.9 4.0 fusion.29
  248.9 4.1 bitcast_add_fusion
  260.1 16.5 %conditional.11 = (f32[256,2,8,128]{3,0,2,1:T(8,128)}, f32[1,256,2,128]{3,1,2,0:T(8,128)S(1)}, f32[1,256,2,128]{3,1,2,0:T(8,128)S(1)}) conditional(s32[]{:T(128)} %convert_element_type.86, f32[256,2,8,128]{3,0,2,1:T(8,128)} %bitcast.186, (s32[]{:T(128)}, s32[256]{0:T(256)S(1)}, s32[16,16]{1,0:T(8,128)S(1)}, bf16[16,256,2,128]{3,1,2,0:T(8,128)(2,1)}, ...), branch_computations={%region_20.20_spmd, %region_21.21_spmd} | conditional | flops 1353974016 | bytes 53599828 | solution.py:203
  260.3 3.6 fusion.44
  266.0 4.0 fusion.29
  270.0 4.1 bitcast_add_fusion
  329.4 4.4 copy.115
  333.9 4.4 copy.114
  350.3 2.0 gather_fusion
  352.3 3.9 bitcast_select_fusion.1
  356.2 233.4 %all_to_all.10 = bf16[16,32,2048]{2,1,0:T(8,128)(2,1)} all-to-all(bf16[16,32,2048]{2,1,0:T(8,128)(2,1)S(1)} %get-tuple-element.1093), channel_id=1, replica_groups=mesh['ctx'=16,'head'=2,'dp'=4] {'ctx'}, dimensions={0} | all-to-all | bytes 4194304 | tf_op jit(solution)/shard_map/all_to_all | solution.py:256
  589.6 6.1 all-to-all-start
  596.6 3.2 gather_fusion.4
  599.8 25.7 %all-to-all-done = bf16[16,32,2048]{2,1,0:T(8,128)(2,1)S(1)} async-done(((bf16[16,32,2048]{2,1,0:T(8,128)(2,1)}), bf16[16,32,2048]{2,1,0:T(8,128)(2,1)S(1)}, u32[]{:S(2)}, u32[]{:S(2)}) %all-to-all-start) | async-done | bytes 2097184 | tf_op jit(solution)/shard_map/all_to_all | solution.py:255
  627.1 36.5 %reduce-scatter.3.cloned.1.call-done = f32[256,256]{1,0:T(8,128)} async-done(((f32[4096,256]{1,0:T(8,128)}), f32[256,256]{1,0:T(8,128)}) %reduce-scatter.3.cloned.1.call-update) | async-done | bytes 262160 | tf_op jit(solution)/shard_map/reduce_scatter | solution.py:228
  665.3 78.8 %reduce-scatter.5.cloned.1.call-done = f32[256,256]{1,0:T(8,128)} async-done(((f32[4096,256]{1,0:T(8,128)}), f32[256,256]{1,0:T(8,128)}) %reduce-scatter.5.cloned.1.call-update) | async-done | bytes 262160 | tf_op jit(solution)/shard_map/reduce_scatter | solution.py:234
  (454 shorter events, 189.0 us)
Async XLA Ops:
  7.2 5.0 copy-start.7
  7.2 49.1 %all-gather.3.cloned.1.call-start = ((), (), s32[]{:S(2)}) async-start(), calls=%async_computation.4 | async-start | bytes 2228224 | tf_op jit(solution)/shard_map/all_gather | solution.py:50
  7.9 135.4 %all-gather.5.cloned.1.call-start = ((), (), s32[]{:S(2)}) async-start(), calls=%async_computation.5 | async-start | bytes 2228224 | tf_op jit(solution)/shard_map/all_gather | solution.py:51
  8.7 655.0 %reduce-scatter.3.cloned.1.call-start = ((), (), s32[]{:S(2)}) async-start(), calls=%async_computation.6 | async-start | bytes 4456448 | tf_op jit(solution)/shard_map/reduce_scatter | solution.py:228
  58.9 2.5 copy-start
  215.2 3.1 copy-start.5
  218.3 3.2 copy-start.2
  248.9 4.9 copy-start.1
  253.0 1.2 copy-start.3
  270.0 4.9 copy-start.1
  274.2 1.2 copy-start.3
  333.9 410.2 %reduce-scatter.5.cloned.1.call-start = ((), (), s32[]{:S(2)}) async-start(), calls=%async_computation.7 | async-start | bytes 4456448 | tf_op jit(solution)/shard_map/reduce_scatter | solution.py:234
  338.3 0.7 copy-start.6
  341.9 3.2 copy-start.4
  589.6 36.0 %all-to-all-start = ((bf16[16,32,2048]{2,1,0:T(8,128)(2,1)}), bf16[16,32,2048]{2,1,0:T(8,128)(2,1)S(1)}, u32[]{:S(2)}, u32[]{:S(2)}) async-start(bf16[16,32,2048]{2,1,0:T(8,128)(2,1)} %get-tuple-element.1094), calls=%async_computation | async-start | bytes 4194304 | tf_op jit(solution)/shard_map/all_to_all | solution.py:255
Sparse Core Ops, SparseCore 0:
  10.2 46.1 all-gather.2
  58.4 44.2 all-gather.4
  334.0 329.6 reduce-scatter.2
  667.2 76.8 reduce-scatter.4
where the time goes:
time: 759 us; the launch traced here: 752 us
  blocking collectives  233 us (31%)
  waiting for transfers between devices  187 us (25%)
  local copies, waits for them, and re-layouts  111 us (15%)
  other arithmetic  96.3 us (13%)
  loops' own time  64.2 us (8%)
  matrix products  40.9 us (5%)
  between operations  14 us (2%)
    all_to_all x1, blocking collectives, shards(): lax.all_to_all(pack(grad_rows), 'ctx', split_axis=0, concat_axis=0, tiled...  233 us
    reduce_scatter x1, waiting for transfers between devices, shards(): lax.psum_scatter(grad_value_terms.reshape(devices * tok_rows, key_width),...  78.8 us
    all_gather x1, waiting for transfers between devices, shards(): lax.all_gather(key_matrix, 'ctx', axis=0, tiled=True)  44 us
    reduce_scatter x1, waiting for transfers between devices, shards(): lax.psum_scatter(grad_key_terms.reshape(devices * tok_rows, key_width), '...  36.5 us
    le x48, other arithmetic, tile_seen(): piece_first <= tile_pos  34.9 us
    reduce_or x48, other arithmetic, tile_seen(): jnp.any((piece_first <= tile_pos) & (piece_first + tok_rows - 1 >= tile_s...  31 us
    dynamic_slice x48, local copies, waits for them, and re-layouts, shards(): lax.scan(stats_piece, initial, (key_pieces, piece_starts))  29 us
    all_to_all x1, waiting for transfers between devices, shards(): lax.all_to_all(pack(out_rows), 'ctx', split_axis=0, concat_axis=0, tiled=...  25.7 us
  transfers between devices with their start and end apart: 5, of which 4 were waited for; matrix products, arithmetic and copies ran while one was open for 13% of the time, Pallas kernels for 0%

commit v1 on v0

v1 whole, which is shorter than its diff:
```python
import functools
import math

import jax
import jax.numpy as jnp
from jax import lax
from jax.experimental import pallas as pl
from jax.experimental.pallas import tpu as pltpu
from jax.sharding import PartitionSpec as P

D = 128
BLK = 16
MAX_DOC = 2304
CAP = 2
CHUNK = 4
F32 = jnp.float32
BF16 = jnp.bfloat16


def dot_nt(a, b):
    return lax.dot_general(a, b, (((1,), (1,)), ((), ())), preferred_element_type=F32)


def dot_nn(a, b):
    return lax.dot_general(a, b, (((1,), (0,)), ((), ())), preferred_element_type=F32)


def tables_kernel(n, bpd, me_ref, dest_ref, src_ref, want_ref, count):
    me = me_ref[0]
    for t in range(n * CAP):
        src_ref[t] = 0
    for t in range(n):
        count[t] = 0

    def own_block(b, carry):
        target = dest_ref[me * bpd + b] // bpd
        rank = count[target]
        src_ref[target * CAP + rank] = b
        count[target] = rank + 1
        return carry

    lax.fori_loop(0, bpd, own_block, 0)

    def shard(s, carry):
        def block(b, rank):
            dest = dest_ref[s * bpd + b]
            mine = dest // bpd == me

            @pl.when(mine)
            def _():
                want_ref[dest % bpd] = s * CAP + rank

            return rank + jnp.where(mine, 1, 0)

        lax.fori_loop(0, bpd, block, 0)
        return carry

    lax.fori_loop(0, n, shard, 0)


def main_kernel(
    n,
    pieces,
    lens_ref,
    src_ref,
    want_ref,
    q_ref,
    do_ref,
    k_ref,
    v_ref,
    out_ref,
    dq_ref,
    dk_ref,
    dv_ref,
    kv,
    kt,
    vt,
    bias,
    s_scr,
    p_scr,
    ds_scr,
    acc_k,
    acc_v,
    blocks,
    send,
    g_send,
    g_recv,
    kv_ssem,
    kv_rsem,
    g_ssem,
    g_rsem,
    a_ssem,
    a_rsem,
    *recv,
):
    me = lax.axis_index("ctx")
    tok, width = q_ref.shape
    heads = width // D
    groups = k_ref.shape[1] // D
    per_group = heads // groups
    chunks = heads // CHUNK
    chunks_group = chunks // groups
    bpd = tok // BLK
    scale = 1.0 / math.sqrt(D)
    log2e_scale = scale * math.log2(math.e)

    barrier = pltpu.get_barrier_semaphore()
    for o in range(1, n):
        pl.semaphore_signal(
            barrier,
            inc=1,
            device_id={"ctx": lax.rem(me + o, n)},
            device_id_type=pl.DeviceIdType.MESH,
        )

    for g in range(groups):
        kv[0, g, 0] = k_ref[:, g * D : (g + 1) * D]
        kv[0, g, 1] = v_ref[:, g * D : (g + 1) * D]
    for d in range(1, pieces):

        @pl.when(me < d)
        def _(d=d):
            kv[d] = jnp.zeros_like(kv[d])

    pl.semaphore_wait(barrier, n - 1)

    def kv_copy(d, g):
        return pltpu.make_async_remote_copy(
            src_ref=kv.at[0, g],
            dst_ref=kv.at[d, g],
            send_sem=kv_ssem.at[d, g],
            recv_sem=kv_rsem.at[d, g],
            device_id={"ctx": lax.rem(me + d, n)},
            device_id_type=pl.DeviceIdType.MESH,
        )

    def grad_copy(d, g):
        return pltpu.make_async_remote_copy(
            src_ref=g_send.at[d, g],
            dst_ref=g_recv.at[d, g],
            send_sem=g_ssem.at[d, g],
            recv_sem=g_rsem.at[d, g],
            device_id={"ctx": lax.rem(me + n - d, n)},
            device_id_type=pl.DeviceIdType.MESH,
        )

    for g in range(groups):
        for d in range(1, pieces):

            @pl.when(me + d < n)
            def _(d=d, g=g):
                kv_copy(d, g).start()

    acc_k[...] = jnp.zeros_like(acc_k)
    acc_v[...] = jnp.zeros_like(acc_v)
    query_pos = me * tok + lax.broadcasted_iota(jnp.int32, (1, tok), 1)
    end = jnp.int32(0)
    start = jnp.zeros((1, tok), jnp.int32)
    for doc in range(lens_ref.shape[0]):
        end = end + lens_ref[doc]
        start = start + jnp.where(end <= query_pos, lens_ref[doc], 0)
    for p in range(pieces):
        key_pos = (me - p) * tok + lax.broadcasted_iota(jnp.int32, (tok, tok), 0)
        seen = (key_pos >= start) & (key_pos <= query_pos)
        bias[p] = jnp.where(seen, 0.0, -jnp.inf).astype(F32)

    def fold(x, op):
        return op(x.reshape(tok // 8, 8, tok), axis=0)

    def head_step(ch, g, j):
        h = ch * CHUNK + j
        cols = pl.ds(pl.multiple_of(h * D, D), D)
        q = q_ref[:, cols]
        do = do_ref[:, cols]
        peak = None
        for p in range(pieces):
            s = dot_nt(kv[p, g, 0], q) + bias[p]
            s_scr[p] = s
            top = fold(s, jnp.max)
            peak = top if peak is None else jnp.maximum(peak, top)
        peak = jnp.max(peak, axis=0, keepdims=True)
        total = None
        for p in range(pieces):
            e = jnp.exp2((s_scr[p] - peak) * log2e_scale)
            s_scr[p] = e
            p_scr[p * tok : (p + 1) * tok] = e.astype(BF16)
            part = fold(e, jnp.sum)
            total = part if total is None else total + part
        inv = 1.0 / jnp.sum(total, axis=0, keepdims=True)
        out_t = (dot_nn(vt[g], p_scr[...]) * inv).astype(BF16).astype(F32)
        delta = jnp.sum(out_t * do.astype(F32).T, axis=0, keepdims=True)
        lanes = pl.ds(pl.multiple_of(j * D, D), D)
        blocks[0, :, :, lanes] = out_t.T.astype(BF16).reshape(bpd, BLK, D)
        for p in range(pieces):
            dp = dot_nt(kv[p, g, 1], do)
            pn = s_scr[p] * inv
            ds = (pn * (dp - delta)).astype(BF16)
            ds_scr[p * tok : (p + 1) * tok] = ds
            acc_v[g, p] += dot_nn(pn.astype(BF16), do)
            acc_k[g, p] += dot_nn(ds, q)
        dq_t = dot_nn(kt[g], ds_scr[...]) * scale
        blocks[1, :, :, lanes] = dq_t.T.astype(BF16).reshape(bpd, BLK, D)

    def block_copy(ch, o):
        target = lax.rem(me + o, n)
        return pltpu.make_async_remote_copy(
            src_ref=send.at[ch, target],
            dst_ref=recv[ch].at[me],
            send_sem=a_ssem.at[ch],
            recv_sem=a_rsem.at[ch],
            device_id={"ctx": target},
            device_id_type=pl.DeviceIdType.MESH,
        )

    def chunk_step(ch, carry):
        g = ch // chunks_group
        first = lax.rem(ch, chunks_group) == 0
        last = lax.rem(ch, chunks_group) == chunks_group - 1

        @pl.when(first)
        def _():
            for d in range(pieces):
                if d > 0:

                    @pl.when(me >= d)
                    def _(d=d):
                        kv_copy(d, g).wait_recv()

                kt[g, :, d * tok : (d + 1) * tok] = kv[d, g, 0].astype(F32).T.astype(BF16)
                vt[g, :, d * tok : (d + 1) * tok] = kv[d, g, 1].astype(F32).T.astype(BF16)

        def one_head(j, inner):
            head_step(ch, g, j)
            return inner

        lax.fori_loop(0, CHUNK, one_head, 0)

        for t in range(n):
            for c in range(CAP):
                b = src_ref[t * CAP + c]
                send[ch, t, c, 0] = blocks[0, b]
                send[ch, t, c, 1] = blocks[1, b]
        for cc in range(chunks):

            @pl.when(ch == cc)
            def _(cc=cc):
                recv[cc][me] = send[cc, me]
                for o in range(1, n):
                    block_copy(cc, o).start()

        @pl.when(last)
        def _():
            for d in range(1, pieces):

                @pl.when(me >= d)
                def _(d=d):
                    g_send[d, g, 0] = acc_k[g, d].astype(BF16)
                    g_send[d, g, 1] = acc_v[g, d].astype(BF16)
                    grad_copy(d, g).start()

        return carry

    lax.fori_loop(0, chunks, chunk_step, 0)

    for ch in range(chunks):
        held = recv[ch].at[pl.ds(0, n - 1)]
        pltpu.make_async_copy(held, held, a_rsem.at[ch]).wait()
        for slot in range(bpd):
            w = want_ref[slot]
            rows = slice(slot * BLK, (slot + 1) * BLK)
            cols = slice(ch * CHUNK * D, (ch + 1) * CHUNK * D)
            out_ref[rows, cols] = recv[ch][w // CAP, w % CAP, 0]
            dq_ref[rows, cols] = recv[ch][w // CAP, w % CAP, 1]

    for g in range(groups):
        for d in range(1, pieces):

            @pl.when(me + d < n)
            def _(d=d, g=g):
                grad_copy(d, g).wait_recv()
                acc_k[g, 0] += g_recv[d, g, 0].astype(F32)
                acc_v[g, 0] += g_recv[d, g, 1].astype(F32)

        dk_ref[:, g * D : (g + 1) * D] = (acc_k[g, 0] * scale).astype(BF16)
        dv_ref[:, g * D : (g + 1) * D] = acc_v[g, 0].astype(BF16)

    for ch in range(chunks):
        sent = send.at[ch, pl.ds(0, n - 1)]
        pltpu.make_async_copy(sent, sent, a_ssem.at[ch]).wait()
    for g in range(groups):
        for d in range(1, pieces):

            @pl.when(me + d < n)
            def _(d=d, g=g):
                kv_copy(d, g).wait_send()

            @pl.when(me >= d)
            def _(d=d, g=g):
                grad_copy(d, g).wait_send()


def shards(q, k, v, do, lens, dest):
    n = lax.axis_size("ctx")
    tok, width = q.shape
    heads = width // D
    groups = k.shape[1] // D
    bpd = tok // BLK
    pieces = min(n, (MAX_DOC - 1 + tok - 1) // tok + 1)
    chunks = heads // CHUNK
    keys = pieces * tok
    smem = pl.BlockSpec(memory_space=pltpu.SMEM)
    vmem = pl.BlockSpec(memory_space=pltpu.VMEM)
    me = lax.axis_index("ctx").astype(jnp.int32).reshape(1)
    src, want = pl.pallas_call(
        functools.partial(tables_kernel, n, bpd),
        out_shape=(
            jax.ShapeDtypeStruct((n * CAP,), jnp.int32),
            jax.ShapeDtypeStruct((bpd,), jnp.int32),
        ),
        in_specs=[smem, smem],
        out_specs=(smem, smem),
        scratch_shapes=[pltpu.SMEM((n,), jnp.int32)],
    )(me, dest)
    return pl.pallas_call(
        functools.partial(main_kernel, n, pieces),
        out_shape=(
            jax.ShapeDtypeStruct(q.shape, BF16),
            jax.ShapeDtypeStruct(q.shape, BF16),
            jax.ShapeDtypeStruct(k.shape, BF16),
            jax.ShapeDtypeStruct(v.shape, BF16),
        ),
        in_specs=[smem, smem, smem, vmem, vmem, vmem, vmem],
        out_specs=(vmem, vmem, vmem, vmem),
        scratch_shapes=[
            pltpu.VMEM((pieces, groups, 2, tok, D), BF16),
            pltpu.VMEM((groups, D, keys), BF16),
            pltpu.VMEM((groups, D, keys), BF16),
            pltpu.VMEM((pieces, tok, tok), F32),
            pltpu.VMEM((pieces, tok, tok), F32),
            pltpu.VMEM((keys, tok), BF16),
            pltpu.VMEM((keys, tok), BF16),
            pltpu.VMEM((groups, pieces, tok, D), F32),
            pltpu.VMEM((groups, pieces, tok, D), F32),
            pltpu.VMEM((2, bpd, BLK, CHUNK * D), BF16),
            pltpu.VMEM((chunks, n, CAP, 2, BLK, CHUNK * D), BF16),
            pltpu.VMEM((pieces, groups, 2, tok, D), BF16),
            pltpu.VMEM((pieces, groups, 2, tok, D), BF16),
            pltpu.SemaphoreType.DMA((pieces, groups)),
            pltpu.SemaphoreType.DMA((pieces, groups)),
            pltpu.SemaphoreType.DMA((pieces, groups)),
            pltpu.SemaphoreType.DMA((pieces, groups)),
            pltpu.SemaphoreType.DMA((chunks,)),
            pltpu.SemaphoreType.DMA((chunks,)),
        ]
        + [pltpu.VMEM((n, CAP, 2, BLK, CHUNK * D), BF16)] * chunks,
        compiler_params=pltpu.CompilerParams(
            collective_id=0, has_side_effects=True, vmem_limit_bytes=60 * 2**20
        ),
    )(lens, src, want, q, do, k, v)


def solution(mesh):
    rows = P(("dp", "ctx"), "head")
    return jax.shard_map(
        shards,
        mesh=mesh,
        in_specs=(rows, rows, rows, rows, P("dp"), P("dp")),
        out_specs=(rows, rows, rows, rows),
        check_vma=False,
    )
```

time: 759 us -> 159 us (0.21)
  blocking collectives: 233 us -> 0 us
  waiting for transfers between devices: 187 us -> 0 us
  Pallas kernels: 0 us -> 153 us
  local copies, waits for them, and re-layouts: 111 us -> 5.02 us
  other arithmetic: 96.3 us -> 0 us
  loops' own time: 64.2 us -> 0 us
  matrix products: 40.9 us -> 0 us
  between operations: 14 us -> 0.66 us
    all_to_all x1 -> x0, blocking collectives: 233 us -> none  [shards(): lax.all_to_all(pack(grad_rows), 'ctx', split_axis=0, concat_axis=0, tiled...]
    pallas_call x0 -> x2, Pallas kernels: none -> 153 us  [the longest x1 148 us: shards(): pl.pallas_call(functools.partial(main_kernel, n, pieces), out_shape=(jax....]
    reduce_scatter x2 -> x0, waiting for transfers between devices: 115 us -> none  [the longest x1 78.8 us: shards(): lax.psum_scatter(grad_value_terms.reshape(devices * tok_rows, key_width),...]
    another operation x51 -> x0, loops' own time: 64.2 us -> none  [the longest x1 22.1 us: shards(): lax.scan(stats_piece, initial, (key_pieces, piece_starts))]
    all_gather x2 -> x0, waiting for transfers between devices: 44.1 us -> none  [the longest x1 44 us: shards(): lax.all_gather(key_matrix, 'ctx', axis=0, tiled=True)]
    dot_general x14 -> x0, matrix products: 40.9 us -> none  [the longest x2 9.86 us: value_tile(): jnp.einsum('gjrp,pgd->gjrd', probs_low, value_piece, preferred_element_ty...]
    le x48 -> x0, other arithmetic: 34.9 us -> none  [tile_seen(): piece_first <= tile_pos]
    reduce_or x49 -> x0, other arithmetic: 31.2 us -> none  [the longest x48 31 us: tile_seen(): jnp.any((piece_first <= tile_pos) & (piece_first + tok_rows - 1 >= tile_s...]
  transfers between devices with their start and end apart: 5 -> 0, of which waited for: 4 -> 0; matrix products, arithmetic and copies ran while one was open for 13% -> 0% of each run, Pallas kernels for 0% -> 0%
where the time goes in v1:
time: 159 us
  Pallas kernels  153 us (96%)
  local copies, waits for them, and re-layouts  5.02 us (3%)
    pallas_call x1, Pallas kernels, shards(): pl.pallas_call(functools.partial(main_kernel, n, pieces), out_shape=(jax....  148 us
    pallas_call x1, Pallas kernels, shards(): pl.pallas_call(functools.partial(tables_kernel, n, bpd), out_shape=(jax.S...  5.12 us
    unnamed x10, local copies, waits for them, and re-layouts  5.02 us

profile of v1, /device:TPU:66, one launch (start us, length us, event | category | flops | bytes accessed | tf_op | source)
XLA Modules:
  0.0 158.9 jit_solution(9729053939526071083)
XLA Ops:
  0.6 5.1 %shard_map.93 = (s32[32]{0:T(128)}, s32[16]{0:T(128)}) custom-call(s32[1]{0:T(128)} %bitcast.me_ref, s32[256]{0:T(256)} %dest_ref.1), custom_call_target="tpu_custom_call" | custom-call | tf_op jit(solution)/shard_map/pallas_call | solution.py:314
  5.8 148.1 %shard_map.94 = (bf16[256,2048]{1,0:T(8,128)(2,1)}, bf16[256,2048]{1,0:T(8,128)(2,1)}, bf16[256,256]{1,0:T(8,128)(2,1)}, bf16[256,256]{1,0:T(8,128)(2,1)}) custom-call(s32[8]{0:T(128)} %lens_ref.1, s32[32]{0:T(128)} %get-tuple-element.6.src_ref, s32[16]{0:T(128)} %get-tuple-element.7.want_ref, bf16[256,2048]{1,0:T(8,128)(2,1)} %q_ref.1, ...), custom_call_target="tpu_custom_call" | custom-call | tf_op jit(solution)/shard_map/pallas_call | solution.py:324
  153.9 0.0 copy-start
  153.9 2.4 %copy.14 = bf16[256,2048]{1,0:T(8,128)(2,1)} copy(bf16[256,2048]{1,0:T(8,128)(2,1)} %get-tuple-element.12) | data formatting | bytes 2097152
  156.3 0.0 copy-done
  156.3 0.0 copy-start.2
  156.3 1.0 copy.15
  157.2 0.1 copy-done.2
  157.3 0.0 copy-start.1
  157.3 0.7 copy.16
  158.0 0.3 copy-done.1
  158.2 0.7 copy.17
Async XLA Ops:
  153.9 2.4 %copy-start = (bf16[256,2048]{1,0:T(8,128)(2,1)S(1)}, bf16[256,2048]{1,0:T(8,128)(2,1)}, u32[]{:S(2)}) copy-start(bf16[256,2048]{1,0:T(8,128)(2,1)} %get-tuple-element.13) | copy-start | bytes 3145732
  156.3 1.0 copy-start.2
  157.3 1.0 copy-start.1

commit v2 on v1

--- a/solution.py
+++ b/solution.py
@@ -12,7 +12,8 @@
 BLK = 16
 MAX_DOC = 2304
 CAP = 2
-CHUNK = 4
+CHUNK = 2
+ROW = 4
 F32 = jnp.float32
 BF16 = jnp.bfloat16
 
@@ -23,47 +24,13 @@
 
 def dot_nn(a, b):
     return lax.dot_general(a, b, (((1,), (0,)), ((), ())), preferred_element_type=F32)
-
-
-def tables_kernel(n, bpd, me_ref, dest_ref, src_ref, want_ref, count):
-    me = me_ref[0]
-    for t in range(n * CAP):
-        src_ref[t] = 0
-    for t in range(n):
-        count[t] = 0
-
-    def own_block(b, carry):
-        target = dest_ref[me * bpd + b] // bpd
-        rank = count[target]
-        src_ref[target * CAP + rank] = b
-        count[target] = rank + 1
-        return carry
-
-    lax.fori_loop(0, bpd, own_block, 0)
-
-    def shard(s, carry):
-        def block(b, rank):
-            dest = dest_ref[s * bpd + b]
-            mine = dest // bpd == me
-
-            @pl.when(mine)
-            def _():
-                want_ref[dest % bpd] = s * CAP + rank
-
-            return rank + jnp.where(mine, 1, 0)
-
-        lax.fori_loop(0, bpd, block, 0)
-        return carry
-
-    lax.fori_loop(0, n, shard, 0)
 
 
 def main_kernel(
     n,
     pieces,
     lens_ref,
-    src_ref,
-    want_ref,
+    dest_ref,
     q_ref,
     do_ref,
     k_ref,
@@ -91,6 +58,9 @@
     g_rsem,
     a_ssem,
     a_rsem,
+    tab_v,
+    tab_s,
+    tab_sem,
     *recv,
 ):
     me = lax.axis_index("ctx")
@@ -113,26 +83,96 @@
             device_id_type=pl.DeviceIdType.MESH,
         )
 
+    x, y = me // ROW, lax.rem(me, ROW)
+    opp = lax.rem(y + ROW // 2, ROW)
+    n_rows = n // ROW
+    base = ROW - 1
     for g in range(groups):
-        kv[0, g, 0] = k_ref[:, g * D : (g + 1) * D]
-        kv[0, g, 1] = v_ref[:, g * D : (g + 1) * D]
+        kv[base, g, 0] = k_ref[:, g * D : (g + 1) * D]
+        kv[base, g, 1] = v_ref[:, g * D : (g + 1) * D]
     for d in range(1, pieces):
 
         @pl.when(me < d)
         def _(d=d):
-            kv[d] = jnp.zeros_like(kv[d])
+            kv[base + d] = jnp.zeros_like(kv[base + d])
 
     pl.semaphore_wait(barrier, n - 1)
 
-    def kv_copy(d, g):
-        return pltpu.make_async_remote_copy(
-            src_ref=kv.at[0, g],
-            dst_ref=kv.at[d, g],
-            send_sem=kv_ssem.at[d, g],
-            recv_sem=kv_rsem.at[d, g],
-            device_id={"ctx": lax.rem(me + d, n)},
-            device_id_type=pl.DeviceIdType.MESH,
-        )
+    def hop(g, message, src, dst, dx, ty, go):
+        @pl.when(go)
+        def _():
+            pltpu.make_async_remote_copy(
+                src_ref=kv.at[base + src, g],
+                dst_ref=kv.at[base + dst, g],
+                send_sem=kv_ssem.at[message, g],
+                recv_sem=kv_rsem.at[base + dst, g],
+                device_id={"ctx": (x + dx) * ROW + ty},
+                device_id_type=pl.DeviceIdType.MESH,
+            ).start()
+
+    def drain(g, message, go):
+        @pl.when(go)
+        def _():
+            held = kv.at[base, g]
+            pltpu.make_async_copy(held, held, kv_ssem.at[message, g]).wait()
+
+    def arrive(g, d, go):
+        @pl.when(go)
+        def _():
+            held = kv.at[base + d, g]
+            pltpu.make_async_copy(held, held, kv_rsem.at[base + d, g]).wait()
+
+    def beside(k):
+        return lax.rem(y + k, ROW)
+
+    below = x < n_rows - 1
+    third = (y == ROW - 1) & (x + 3 < n_rows)
+    row_go = {k: (beside(k) > y) | (below if k == ROW // 2 else (y < 0)) for k in range(1, ROW)}
+    far_opp = (x >= 1) & below & (2 * ROW + y - opp < pieces)
+    far_go = {k: (x >= 2) & (2 * ROW + beside(k) - y < pieces) for k in (1, ROW - 1)}
+
+    def stage_one(g):
+        hop(g, 0, 0, ROW, 1, y, below)
+        for k in range(1, ROW):
+            hop(g, k, 0, beside(k) - y, 0, beside(k), row_go[k])
+        hop(g, ROW, 0, 3 * ROW - y, 3, 0, third)
+
+    def stage_two(g):
+        arrive(g, ROW, x >= 1)
+        hop(g, 5, ROW, 2 * ROW, 1, y, (x >= 1) & below)
+        hop(g, 6, ROW, ROW + beside(1) - y, 0, beside(1), x >= 1)
+        hop(g, 7, ROW, ROW + beside(ROW - 1) - y, 0, beside(ROW - 1), x >= 1)
+        arrive(g, y - opp, below | (y > opp))
+        hop(g, 8, y - opp, ROW + y - opp, 1, y, below)
+
+    def stage_three(g):
+        arrive(g, 2 * ROW, x >= 2)
+        hop(g, 9, 2 * ROW, 2 * ROW + beside(1) - y, 0, beside(1), far_go[1])
+        hop(g, 10, 2 * ROW, 2 * ROW + beside(ROW - 1) - y, 0, beside(ROW - 1), far_go[ROW - 1])
+        arrive(g, ROW + y - opp, x >= 1)
+        hop(g, 11, ROW + y - opp, 2 * ROW + y - opp, 1, y, far_opp)
+
+    def stage_last(g):
+        for k in (1, ROW - 1):
+            side = beside(k)
+            arrive(g, y - side, side < y)
+            arrive(g, ROW + y - side, x >= 1)
+            arrive(g, 2 * ROW + y - side, (x >= 2) & (2 * ROW + y - side < pieces))
+        arrive(g, 2 * ROW + y - opp, (x >= 2) & (2 * ROW + y - opp < pieces))
+        arrive(g, 2 * ROW + 1, (x >= 3) & (y == 0))
+
+    def stage_sent(g):
+        drain(g, 0, below)
+        for k in range(1, ROW):
+            drain(g, k, row_go[k])
+        drain(g, ROW, third)
+        drain(g, 5, (x >= 1) & below)
+        drain(g, 6, x >= 1)
+        drain(g, 7, x >= 1)
+        drain(g, 8, below)
+        drain(g, 9, far_go[1])
+        drain(g, 10, far_go[ROW - 1])
+        drain(g, 11, far_opp)
 
     def grad_copy(d, g):
         return pltpu.make_async_remote_copy(
@@ -144,12 +184,24 @@
             device_id_type=pl.DeviceIdType.MESH,
         )
 
-    for g in range(groups):
-        for d in range(1, pieces):
-
-            @pl.when(me + d < n)
-            def _(d=d, g=g):
-                kv_copy(d, g).start()
+    stage_one(0)
+
+    nb = n * bpd
+    lane = lax.broadcasted_iota(jnp.int32, (nb, nb), 1)
+    sub = lax.broadcasted_iota(jnp.int32, (nb, nb), 0)
+    dest_row = jnp.broadcast_to(dest_ref[...], (nb, nb))
+    dest_col = dest_row.T
+    same = (dest_row // bpd == dest_col // bpd) & (lane // bpd == sub // bpd) & (lane < sub)
+    rank = jnp.sum(jnp.where(same, 1.0, 0.0).astype(F32), axis=1, keepdims=True).astype(jnp.int32)
+    slot = (dest_col // bpd) * CAP + rank
+    picked = (sub // bpd == me) & (slot == lane)
+    src_row = jnp.sum(jnp.where(picked, sub - me * bpd, 0), axis=0, keepdims=True)
+    tab_v[0:1] = jnp.clip(src_row, 0, bpd - 1)
+    found = dest_col == me * bpd + lane
+    want_row = jnp.sum(jnp.where(found, (sub // bpd) * CAP + rank, 0), axis=0, keepdims=True)
+    tab_v[1:2] = jnp.clip(want_row, 0, n * CAP - 1)
+    to_smem = pltpu.make_async_copy(tab_v, tab_s, tab_sem)
+    to_smem.start()
 
     acc_k[...] = jnp.zeros_like(acc_k)
     acc_v[...] = jnp.zeros_like(acc_v)
@@ -164,6 +216,12 @@
         seen = (key_pos >= start) & (key_pos <= query_pos)
         bias[p] = jnp.where(seen, 0.0, -jnp.inf).astype(F32)
 
+    to_smem.wait()
+    stage_two(0)
+    stage_three(0)
+    for g in range(1, groups):
+        stage_one(g)
+
     def fold(x, op):
         return op(x.reshape(tok // 8, 8, tok), axis=0)
 
@@ -174,7 +232,7 @@
         do = do_ref[:, cols]
         peak = None
         for p in range(pieces):
-            s = dot_nt(kv[p, g, 0], q) + bias[p]
+            s = dot_nt(kv[base + p, g, 0], q) + bias[p]
             s_scr[p] = s
             top = fold(s, jnp.max)
             peak = top if peak is None else jnp.maximum(peak, top)
@@ -192,7 +250,7 @@
         lanes = pl.ds(pl.multiple_of(j * D, D), D)
         blocks[0, :, :, lanes] = out_t.T.astype(BF16).reshape(bpd, BLK, D)
         for p in range(pieces):
-            dp = dot_nt(kv[p, g, 1], do)
+            dp = dot_nt(kv[base + p, g, 1], do)
             pn = s_scr[p] * inv
             ds = (pn * (dp - delta)).astype(BF16)
             ds_scr[p * tok : (p + 1) * tok] = ds
@@ -219,15 +277,10 @@
 
         @pl.when(first)
         def _():
+            stage_last(g)
             for d in range(pieces):
-                if d > 0:
-
-                    @pl.when(me >= d)
-                    def _(d=d):
-                        kv_copy(d, g).wait_recv()
-
-                kt[g, :, d * tok : (d + 1) * tok] = kv[d, g, 0].astype(F32).T.astype(BF16)
-                vt[g, :, d * tok : (d + 1) * tok] = kv[d, g, 1].astype(F32).T.astype(BF16)
+                kt[g, :, d * tok : (d + 1) * tok] = kv[base + d, g, 0].astype(F32).T.astype(BF16)
+                vt[g, :, d * tok : (d + 1) * tok] = kv[base + d, g, 1].astype(F32).T.astype(BF16)
 
         def one_head(j, inner):
             head_step(ch, g, j)
@@ -237,7 +290,7 @@
 
         for t in range(n):
             for c in range(CAP):
-                b = src_ref[t * CAP + c]
+                b = tab_s[0, t * CAP + c]
                 send[ch, t, c, 0] = blocks[0, b]
                 send[ch, t, c, 1] = blocks[1, b]
         for cc in range(chunks):
@@ -248,6 +301,16 @@
                 for o in range(1, n):
                     block_copy(cc, o).start()
 
+        for g2 in range(1, groups):
+
+            @pl.when(ch == (g2 - 1) * chunks_group)
+            def _(g2=g2):
+                stage_two(g2)
+
+            @pl.when(ch == (g2 - 1) * chunks_group + 1)
+            def _(g2=g2):
+                stage_three(g2)
+
         @pl.when(last)
         def _():
             for d in range(1, pieces):
@@ -266,7 +329,7 @@
         held = recv[ch].at[pl.ds(0, n - 1)]
         pltpu.make_async_copy(held, held, a_rsem.at[ch]).wait()
         for slot in range(bpd):
-            w = want_ref[slot]
+            w = tab_s[1, slot]
             rows = slice(slot * BLK, (slot + 1) * BLK)
             cols = slice(ch * CHUNK * D, (ch + 1) * CHUNK * D)
             out_ref[rows, cols] = recv[ch][w // CAP, w % CAP, 0]
@@ -288,11 +351,8 @@
         sent = send.at[ch, pl.ds(0, n - 1)]
         pltpu.make_async_copy(sent, sent, a_ssem.at[ch]).wait()
     for g in range(groups):
+        stage_sent(g)
         for d in range(1, pieces):
-
-            @pl.when(me + d < n)
-            def _(d=d, g=g):
-                kv_copy(d, g).wait_send()
 
             @pl.when(me >= d)
             def _(d=d, g=g):
@@ -310,17 +370,6 @@
     keys = pieces * tok
     smem = pl.BlockSpec(memory_space=pltpu.SMEM)
     vmem = pl.BlockSpec(memory_space=pltpu.VMEM)
-    me = lax.axis_index("ctx").astype(jnp.int32).reshape(1)
-    src, want = pl.pallas_call(
-        functools.partial(tables_kernel, n, bpd),
-        out_shape=(
-            jax.ShapeDtypeStruct((n * CAP,), jnp.int32),
-            jax.ShapeDtypeStruct((bpd,), jnp.int32),
-        ),
-        in_specs=[smem, smem],
-        out_specs=(smem, smem),
-        scratch_shapes=[pltpu.SMEM((n,), jnp.int32)],
-    )(me, dest)
     return pl.pallas_call(
         functools.partial(main_kernel, n, pieces),
         out_shape=(
@@ -329,10 +378,10 @@
             jax.ShapeDtypeStruct(k.shape, BF16),
             jax.ShapeDtypeStruct(v.shape, BF16),
         ),
-        in_specs=[smem, smem, smem, vmem, vmem, vmem, vmem],
+        in_specs=[smem, vmem, vmem, vmem, vmem, vmem],
         out_specs=(vmem, vmem, vmem, vmem),
         scratch_shapes=[
-            pltpu.VMEM((pieces, groups, 2, tok, D), BF16),
+            pltpu.VMEM((4 * ROW - 1, groups, 2, tok, D), BF16),
             pltpu.VMEM((groups, D, keys), BF16),
             pltpu.VMEM((groups, D, keys), BF16),
             pltpu.VMEM((pieces, tok, tok), F32),
@@ -345,18 +394,21 @@
             pltpu.VMEM((chunks, n, CAP, 2, BLK, CHUNK * D), BF16),
             pltpu.VMEM((pieces, groups, 2, tok, D), BF16),
             pltpu.VMEM((pieces, groups, 2, tok, D), BF16),
-            pltpu.SemaphoreType.DMA((pieces, groups)),
-            pltpu.SemaphoreType.DMA((pieces, groups)),
+            pltpu.SemaphoreType.DMA((3 * ROW, groups)),
+            pltpu.SemaphoreType.DMA((4 * ROW - 1, groups)),
             pltpu.SemaphoreType.DMA((pieces, groups)),
             pltpu.SemaphoreType.DMA((pieces, groups)),
             pltpu.SemaphoreType.DMA((chunks,)),
             pltpu.SemaphoreType.DMA((chunks,)),
+            pltpu.VMEM((2, n * bpd), jnp.int32),
+            pltpu.SMEM((2, n * bpd), jnp.int32),
+            pltpu.SemaphoreType.DMA(()),
         ]
         + [pltpu.VMEM((n, CAP, 2, BLK, CHUNK * D), BF16)] * chunks,
         compiler_params=pltpu.CompilerParams(
             collective_id=0, has_side_effects=True, vmem_limit_bytes=60 * 2**20
         ),
-    )(lens, src, want, q, do, k, v)
+    )(lens, dest.reshape(1, n * bpd), q, do, k, v)
 
 
 def solution(mesh):

time: 159 us -> 139 us (0.87)
  Pallas kernels: 153 us -> 133 us
    pallas_call x1, Pallas kernels: 148 us -> 133 us  [shards(): pl.pallas_call(functools.partial(main_kernel, n, pieces), out_shape=(jax....]
    pallas_call x1 -> x0, Pallas kernels: 5.12 us -> none  [shards(): pl.pallas_call(functools.partial(tables_kernel, n, bpd), out_shape=(jax.S...]
where the time goes in v2:
time: 139 us
  Pallas kernels  133 us (96%)
  local copies, waits for them, and re-layouts  5.02 us (4%)
    pallas_call x1, Pallas kernels, shards(): pl.pallas_call(functools.partial(main_kernel, n, pieces), out_shape=(jax....  133 us
    unnamed x10, local copies, waits for them, and re-layouts  5.02 us

profile of v2, /device:TPU:66, one launch (start us, length us, event | category | flops | bytes accessed | tf_op | source)
XLA Modules:
  0.0 139.0 jit_solution(15444174241266938905)
XLA Ops:
  0.6 133.3 %shard_map.93 = (bf16[256,2048]{1,0:T(8,128)(2,1)}, bf16[256,2048]{1,0:T(8,128)(2,1)}, bf16[256,256]{1,0:T(8,128)(2,1)}, bf16[256,256]{1,0:T(8,128)(2,1)}) custom-call(s32[8]{0:T(128)} %lens_ref.1, s32[1,256]{1,0:T(1,128)} %bitcast.1, bf16[256,2048]{1,0:T(8,128)(2,1)} %q_ref.1, bf16[256,2048]{1,0:T(8,128)(2,1)} %do_ref.1, bf16[256,256]{1,0:T(8,128)(2,1)} %k_ref.1, ...), custom_call_target="tpu_custom_call" | custom-call | tf_op jit(solution)/shard_map/pallas_call | solution.py:373
  133.9 0.0 copy-start
  134.0 2.4 %copy.14 = bf16[256,2048]{1,0:T(8,128)(2,1)} copy(bf16[256,2048]{1,0:T(8,128)(2,1)} %get-tuple-element.8) | data formatting | bytes 2097152
  136.4 0.0 copy-done
  136.4 0.0 copy-start.2
  136.4 1.0 copy.15
  137.3 0.1 copy-done.2
  137.4 0.0 copy-start.1
  137.4 0.7 copy.16
  138.0 0.3 copy-done.1
  138.3 0.7 copy.17
Async XLA Ops:
  133.9 2.4 %copy-start = (bf16[256,2048]{1,0:T(8,128)(2,1)S(1)}, bf16[256,2048]{1,0:T(8,128)(2,1)}, u32[]{:S(2)}) copy-start(bf16[256,2048]{1,0:T(8,128)(2,1)} %get-tuple-element.9) | copy-start | bytes 3145732
  136.4 1.0 copy-start.2
  137.4 1.0 copy-start.1

commit v3 on v2

--- a/solution.py
+++ b/solution.py
@@ -174,15 +174,113 @@
         drain(g, 10, far_go[ROW - 1])
         drain(g, 11, far_opp)
 
-    def grad_copy(d, g):
-        return pltpu.make_async_remote_copy(
-            src_ref=g_send.at[d, g],
-            dst_ref=g_recv.at[d, g],
-            send_sem=g_ssem.at[d, g],
-            recv_sem=g_rsem.at[d, g],
-            device_id={"ctx": lax.rem(me + n - d, n)},
+    def put(g, message, d):
+        g_send[message, g, 0] = acc_k[g, d].astype(BF16)
+        g_send[message, g, 1] = acc_v[g, d].astype(BF16)
+
+    def ship(g, message, dx, ty):
+        pltpu.make_async_remote_copy(
+            src_ref=g_send.at[message, g],
+            dst_ref=g_recv.at[message, g],
+            send_sem=g_ssem.at[message, g],
+            recv_sem=g_rsem.at[message, g],
+            device_id={"ctx": (x - dx) * ROW + ty},
             device_id_type=pl.DeviceIdType.MESH,
-        )
+        ).start()
+
+    def give(g, message, d, dx, ty, go):
+        @pl.when(go)
+        def _():
+            put(g, message, d)
+            ship(g, message, dx, ty)
+
+    def landed(g, message):
+        held = g_recv.at[message, g]
+        pltpu.make_async_copy(held, held, g_rsem.at[message, g]).wait()
+
+    def take(g, message, d, go):
+        @pl.when(go)
+        def _():
+            landed(g, message)
+            acc_k[g, d] += g_recv[message, g, 0].astype(F32)
+            acc_v[g, d] += g_recv[message, g, 1].astype(F32)
+
+    nxt, prv = beside(1), beside(ROW - 1)
+    opp_go = below | (opp < y)
+    gives = [
+        (x >= 2) & (2 * ROW + y - nxt < pieces),
+        (x >= 2) & (2 * ROW + y - prv < pieces),
+        x >= 1,
+        x >= 1,
+        (x >= 2) & (2 * ROW + y - opp < pieces),
+        nxt < y,
+        prv < y,
+        (x >= 3) & (y == 0),
+        x >= 2,
+        x >= 1,
+        x >= 1,
+        opp_go,
+    ]
+
+    def reduce_one(g):
+        give(g, 0, 2 * ROW + y - nxt, 0, nxt, gives[0])
+        give(g, 1, 2 * ROW + y - prv, 0, prv, gives[1])
+        give(g, 4, 2 * ROW + y - opp, 1, y, gives[4])
+        give(g, 7, 2 * ROW + 1, 3, ROW - 1, gives[7])
+        give(g, 2, ROW + y - nxt, 0, nxt, gives[2])
+        give(g, 3, ROW + y - prv, 0, prv, gives[3])
+        give(g, 5, y - nxt, 0, nxt, gives[5])
+        give(g, 6, y - prv, 0, prv, gives[6])
+
+    def reduce_two(g):
+        take(g, 0, 2 * ROW, (x >= 2) & (2 * ROW + prv - y < pieces))
+        take(g, 1, 2 * ROW, (x >= 2) & (2 * ROW + nxt - y < pieces))
+        give(g, 8, 2 * ROW, 1, y, gives[8])
+
+    def reduce_three(g):
+        take(g, 4, ROW + y - opp, (x >= 1) & below & (2 * ROW + y - opp < pieces))
+        give(g, 10, ROW + y - opp, 1, y, gives[10])
+        take(g, 2, ROW, x >= 1)
+        take(g, 3, ROW, x >= 1)
+        take(g, 8, ROW, (x >= 1) & below)
+        give(g, 9, ROW, 1, y, gives[9])
+
+    def reduce_four(g):
+        @pl.when(opp < y)
+        def _():
+            @pl.when(below)
+            def _():
+                landed(g, 10)
+                acc_k[g, y - opp] += g_recv[10, g, 0].astype(F32)
+                acc_v[g, y - opp] += g_recv[10, g, 1].astype(F32)
+
+            put(g, 11, y - opp)
+
+        @pl.when((opp > y) & below)
+        def _():
+            landed(g, 10)
+            g_send[11, g] = g_recv[10, g]
+
+        @pl.when(opp_go)
+        def _():
+            ship(g, 11, 0, opp)
+
+    def reduce_last(g):
+        take(g, 5, 0, y < prv)
+        take(g, 6, 0, y < nxt)
+        take(g, 7, 0, (y == ROW - 1) & (x + 3 < n_rows))
+        take(g, 9, 0, below)
+        take(g, 11, 0, below | (y < opp))
+        dk_ref[:, g * D : (g + 1) * D] = (acc_k[g, 0] * scale).astype(BF16)
+        dv_ref[:, g * D : (g + 1) * D] = acc_v[g, 0].astype(BF16)
+
+    def reduce_sent(g):
+        for message, go in enumerate(gives):
+
+            @pl.when(go)
+            def _(message=message):
+                held = g_send.at[message, g]
+                pltpu.make_async_copy(held, held, g_ssem.at[message, g]).wait()
 
     stage_one(0)
 
@@ -311,21 +409,21 @@
             def _(g2=g2):
                 stage_three(g2)
 
+            for k, stage in enumerate((reduce_two, reduce_three, reduce_four)):
+
+                @pl.when(ch == g2 * chunks_group + k)
+                def _(g2=g2, stage=stage):
+                    stage(g2 - 1)
+
         @pl.when(last)
         def _():
-            for d in range(1, pieces):
-
-                @pl.when(me >= d)
-                def _(d=d):
-                    g_send[d, g, 0] = acc_k[g, d].astype(BF16)
-                    g_send[d, g, 1] = acc_v[g, d].astype(BF16)
-                    grad_copy(d, g).start()
+            reduce_one(g)
 
         return carry
 
     lax.fori_loop(0, chunks, chunk_step, 0)
 
-    for ch in range(chunks):
+    def unpack(ch):
         held = recv[ch].at[pl.ds(0, n - 1)]
         pltpu.make_async_copy(held, held, a_rsem.at[ch]).wait()
         for slot in range(bpd):
@@ -335,28 +433,23 @@
             out_ref[rows, cols] = recv[ch][w // CAP, w % CAP, 0]
             dq_ref[rows, cols] = recv[ch][w // CAP, w % CAP, 1]
 
-    for g in range(groups):
-        for d in range(1, pieces):
-
-            @pl.when(me + d < n)
-            def _(d=d, g=g):
-                grad_copy(d, g).wait_recv()
-                acc_k[g, 0] += g_recv[d, g, 0].astype(F32)
-                acc_v[g, 0] += g_recv[d, g, 1].astype(F32)
-
-        dk_ref[:, g * D : (g + 1) * D] = (acc_k[g, 0] * scale).astype(BF16)
-        dv_ref[:, g * D : (g + 1) * D] = acc_v[g, 0].astype(BF16)
+    reduce_two(groups - 1)
+    for ch in range(chunks // 2):
+        unpack(ch)
+    reduce_three(groups - 1)
+    for g in range(groups - 1):
+        reduce_last(g)
+    reduce_four(groups - 1)
+    for ch in range(chunks // 2, chunks):
+        unpack(ch)
+    reduce_last(groups - 1)
 
     for ch in range(chunks):
         sent = send.at[ch, pl.ds(0, n - 1)]
         pltpu.make_async_copy(sent, sent, a_ssem.at[ch]).wait()
     for g in range(groups):
         stage_sent(g)
-        for d in range(1, pieces):
-
-            @pl.when(me >= d)
-            def _(d=d, g=g):
-                grad_copy(d, g).wait_send()
+        reduce_sent(g)
 
 
 def shards(q, k, v, do, lens, dest):
@@ -392,12 +485,12 @@
             pltpu.VMEM((groups, pieces, tok, D), F32),
             pltpu.VMEM((2, bpd, BLK, CHUNK * D), BF16),
             pltpu.VMEM((chunks, n, CAP, 2, BLK, CHUNK * D), BF16),
-            pltpu.VMEM((pieces, groups, 2, tok, D), BF16),
-            pltpu.VMEM((pieces, groups, 2, tok, D), BF16),
+            pltpu.VMEM((3 * ROW, groups, 2, tok, D), BF16),
+            pltpu.VMEM((3 * ROW, groups, 2, tok, D), BF16),
             pltpu.SemaphoreType.DMA((3 * ROW, groups)),
             pltpu.SemaphoreType.DMA((4 * ROW - 1, groups)),
-            pltpu.SemaphoreType.DMA((pieces, groups)),
-            pltpu.SemaphoreType.DMA((pieces, groups)),
+            pltpu.SemaphoreType.DMA((3 * ROW, groups)),
+            pltpu.SemaphoreType.DMA((3 * ROW, groups)),
             pltpu.SemaphoreType.DMA((chunks,)),
             pltpu.SemaphoreType.DMA((chunks,)),
             pltpu.VMEM((2, n * bpd), jnp.int32),

time: 139 us -> 119 us (0.86)
  Pallas kernels: 133 us -> 113 us
    pallas_call x1, Pallas kernels: 133 us -> 113 us  [shards(): pl.pallas_call(functools.partial(main_kernel, n, pieces), out_shape=(jax....]
where the time goes in v3:
time: 119 us; the launch traced here: 118 us
  Pallas kernels  113 us (95%)
  local copies, waits for them, and re-layouts  5.02 us (4%)
    pallas_call x1, Pallas kernels, shards(): pl.pallas_call(functools.partial(main_kernel, n, pieces), out_shape=(jax....  113 us
    unnamed x10, local copies, waits for them, and re-layouts  5.02 us

profile of v3, /device:TPU:66, one launch (start us, length us, event | category | flops | bytes accessed | tf_op | source)
XLA Modules:
  0.0 118.4 jit_solution(17166474106119688334)
XLA Ops:
  0.6 112.8 %shard_map.93 = (bf16[256,2048]{1,0:T(8,128)(2,1)}, bf16[256,2048]{1,0:T(8,128)(2,1)}, bf16[256,256]{1,0:T(8,128)(2,1)}, bf16[256,256]{1,0:T(8,128)(2,1)}) custom-call(s32[8]{0:T(128)} %lens_ref.1, s32[1,256]{1,0:T(1,128)} %bitcast.1, bf16[256,2048]{1,0:T(8,128)(2,1)} %q_ref.1, bf16[256,2048]{1,0:T(8,128)(2,1)} %do_ref.1, bf16[256,256]{1,0:T(8,128)(2,1)} %k_ref.1, ...), custom_call_target="tpu_custom_call" | custom-call | tf_op jit(solution)/shard_map/pallas_call | solution.py:466
  113.4 0.0 copy-start
  113.4 2.4 %copy.14 = bf16[256,2048]{1,0:T(8,128)(2,1)} copy(bf16[256,2048]{1,0:T(8,128)(2,1)} %get-tuple-element.8) | data formatting | bytes 2097152
  115.8 0.0 copy-done
  115.8 0.0 copy-start.2
  115.8 1.0 copy.15
  116.8 0.1 copy-done.2
  116.8 0.0 copy-start.1
  116.8 0.7 copy.16
  117.5 0.3 copy-done.1
  117.8 0.7 copy.17
Async XLA Ops:
  113.4 2.4 %copy-start = (bf16[256,2048]{1,0:T(8,128)(2,1)S(1)}, bf16[256,2048]{1,0:T(8,128)(2,1)}, u32[]{:S(2)}) copy-start(bf16[256,2048]{1,0:T(8,128)(2,1)} %get-tuple-element.9) | copy-start | bytes 3145732
  115.8 1.0 copy-start.2
  116.8 1.0 copy-start.1

commit v4 on v3

--- a/solution.py
+++ b/solution.py
@@ -323,39 +323,60 @@
     def fold(x, op):
         return op(x.reshape(tok // 8, 8, tok), axis=0)
 
-    def head_step(ch, g, j):
-        h = ch * CHUNK + j
-        cols = pl.ds(pl.multiple_of(h * D, D), D)
-        q = q_ref[:, cols]
-        do = do_ref[:, cols]
-        peak = None
+    def pair_step(ch, g):
+        cols = [pl.ds(pl.multiple_of((ch * CHUNK + j) * D, D), D) for j in range(CHUNK)]
+        qs = [q_ref[:, c] for c in cols]
+        dos = [do_ref[:, c] for c in cols]
+        peaks, totals = [None] * CHUNK, [None] * CHUNK
+
+        def score(j, p):
+            s = dot_nt(kv[base + p, g, 0], qs[j]) + bias[p]
+            s_scr[j, p] = s
+            top = fold(s, jnp.max)
+            peaks[j] = top if p == 0 else jnp.maximum(peaks[j], top)
+
+        def weigh(j, p):
+            e = jnp.exp2((s_scr[j, p] - peaks[j]) * log2e_scale)
+            s_scr[j, p] = e
+            p_scr[j, p * tok : (p + 1) * tok] = e.astype(BF16)
+            part = fold(e, jnp.sum)
+            totals[j] = part if p == 0 else totals[j] + part
+
+        invs, deltas = [None] * CHUNK, [None] * CHUNK
+
+        def attend(j):
+            invs[j] = 1.0 / jnp.sum(totals[j], axis=0, keepdims=True)
+            out_t = (dot_nn(vt[g], p_scr[j]) * invs[j]).astype(BF16).astype(F32)
+            deltas[j] = jnp.sum(out_t * dos[j].astype(F32).T, axis=0, keepdims=True)
+            blocks[0, :, :, j * D : (j + 1) * D] = out_t.T.astype(BF16).reshape(bpd, BLK, D)
+
+        for j in range(CHUNK):
+            for p in range(pieces):
+                score(j, p)
+                if j > 0:
+                    weigh(j - 1, p)
+            peaks[j] = jnp.max(peaks[j], axis=0, keepdims=True)
+            if j > 0:
+                attend(j - 1)
         for p in range(pieces):
-            s = dot_nt(kv[base + p, g, 0], q) + bias[p]
-            s_scr[p] = s
-            top = fold(s, jnp.max)
-            peak = top if peak is None else jnp.maximum(peak, top)
-        peak = jnp.max(peak, axis=0, keepdims=True)
-        total = None
+            weigh(CHUNK - 1, p)
+        attend(CHUNK - 1)
+        do_cat = jnp.concatenate(dos, axis=0)
+        q_cat = jnp.concatenate(qs, axis=0)
         for p in range(pieces):
-            e = jnp.exp2((s_scr[p] - peak) * log2e_scale)
-            s_scr[p] = e
-            p_scr[p * tok : (p + 1) * tok] = e.astype(BF16)
-            part = fold(e, jnp.sum)
-            total = part if total is None else total + part
-        inv = 1.0 / jnp.sum(total, axis=0, keepdims=True)
-        out_t = (dot_nn(vt[g], p_scr[...]) * inv).astype(BF16).astype(F32)
-        delta = jnp.sum(out_t * do.astype(F32).T, axis=0, keepdims=True)
-        lanes = pl.ds(pl.multiple_of(j * D, D), D)
-        blocks[0, :, :, lanes] = out_t.T.astype(BF16).reshape(bpd, BLK, D)
-        for p in range(pieces):
-            dp = dot_nt(kv[base + p, g, 1], do)
-            pn = s_scr[p] * inv
-            ds = (pn * (dp - delta)).astype(BF16)
-            ds_scr[p * tok : (p + 1) * tok] = ds
-            acc_v[g, p] += dot_nn(pn.astype(BF16), do)
-            acc_k[g, p] += dot_nn(ds, q)
-        dq_t = dot_nn(kt[g], ds_scr[...]) * scale
-        blocks[1, :, :, lanes] = dq_t.T.astype(BF16).reshape(bpd, BLK, D)
+            pns, dss = [], []
+            for j in range(CHUNK):
+                dp = dot_nt(kv[base + p, g, 1], dos[j])
+                pn = s_scr[j, p] * invs[j]
+                ds = (pn * (dp - deltas[j])).astype(BF16)
+                ds_scr[j, p * tok : (p + 1) * tok] = ds
+                dss.append(ds)
+                pns.append(pn.astype(BF16))
+            acc_v[g, p] += dot_nn(jnp.concatenate(pns, axis=1), do_cat)
+            acc_k[g, p] += dot_nn(jnp.concatenate(dss, axis=1), q_cat)
+        for j in range(CHUNK):
+            dq_t = dot_nn(kt[g], ds_scr[j]) * scale
+            blocks[1, :, :, j * D : (j + 1) * D] = dq_t.T.astype(BF16).reshape(bpd, BLK, D)
 
     def block_copy(ch, o):
         target = lax.rem(me + o, n)
@@ -380,11 +401,11 @@
                 kt[g, :, d * tok : (d + 1) * tok] = kv[base + d, g, 0].astype(F32).T.astype(BF16)
                 vt[g, :, d * tok : (d + 1) * tok] = kv[base + d, g, 1].astype(F32).T.astype(BF16)
 
-        def one_head(j, inner):
-            head_step(ch, g, j)
-            return inner
-
-        lax.fori_loop(0, CHUNK, one_head, 0)
+        pair_step(ch, g)
+
+        @pl.when(last)
+        def _():
+            reduce_one(g)
 
         for t in range(n):
             for c in range(CAP):
@@ -411,13 +432,9 @@
 
             for k, stage in enumerate((reduce_two, reduce_three, reduce_four)):
 
-                @pl.when(ch == g2 * chunks_group + k)
+                @pl.when(ch == g2 * chunks_group + k + 1)
                 def _(g2=g2, stage=stage):
                     stage(g2 - 1)
-
-        @pl.when(last)
-        def _():
-            reduce_one(g)
 
         return carry
 
@@ -434,13 +451,11 @@
             dq_ref[rows, cols] = recv[ch][w // CAP, w % CAP, 1]
 
     reduce_two(groups - 1)
-    for ch in range(chunks // 2):
-        unpack(ch)
     reduce_three(groups - 1)
     for g in range(groups - 1):
         reduce_last(g)
     reduce_four(groups - 1)
-    for ch in range(chunks // 2, chunks):
+    for ch in range(chunks):
         unpack(ch)
     reduce_last(groups - 1)
 
@@ -478,9 +493,9 @@
             pltpu.VMEM((groups, D, keys), BF16),
             pltpu.VMEM((groups, D, keys), BF16),
             pltpu.VMEM((pieces, tok, tok), F32),
-            pltpu.VMEM((pieces, tok, tok), F32),
-            pltpu.VMEM((keys, tok), BF16),
-            pltpu.VMEM((keys, tok), BF16),
+            pltpu.VMEM((CHUNK, pieces, tok, tok), F32),
+            pltpu.VMEM((CHUNK, keys, tok), BF16),
+            pltpu.VMEM((CHUNK, keys, tok), BF16),
             pltpu.VMEM((groups, pieces, tok, D), F32),
             pltpu.VMEM((groups, pieces, tok, D), F32),
             pltpu.VMEM((2, bpd, BLK, CHUNK * D), BF16),

time: 119 us -> 112 us (0.941)
  Pallas kernels: 113 us -> 106 us
    pallas_call x1, Pallas kernels: 113 us -> 106 us  [shards(): pl.pallas_call(functools.partial(main_kernel, n, pieces), out_shape=(jax....]
where the time goes in v4:
time: 112 us; the launch traced here: 111 us
  Pallas kernels  106 us (95%)
  local copies, waits for them, and re-layouts  5.02 us (4%)
    pallas_call x1, Pallas kernels, shards(): pl.pallas_call(functools.partial(main_kernel, n, pieces), out_shape=(jax....  106 us
    unnamed x10, local copies, waits for them, and re-layouts  5.02 us

profile of v4, /device:TPU:66, one launch (start us, length us, event | category | flops | bytes accessed | tf_op | source)
XLA Modules:
  0.0 111.3 jit_solution(13323561884251077769)
XLA Ops:
  0.6 105.7 %shard_map.93 = (bf16[256,2048]{1,0:T(8,128)(2,1)}, bf16[256,2048]{1,0:T(8,128)(2,1)}, bf16[256,256]{1,0:T(8,128)(2,1)}, bf16[256,256]{1,0:T(8,128)(2,1)}) custom-call(s32[8]{0:T(128)} %lens_ref.1, s32[1,256]{1,0:T(1,128)} %bitcast.1, bf16[256,2048]{1,0:T(8,128)(2,1)} %q_ref.1, bf16[256,2048]{1,0:T(8,128)(2,1)} %do_ref.1, bf16[256,256]{1,0:T(8,128)(2,1)} %k_ref.1, ...), custom_call_target="tpu_custom_call" | custom-call | tf_op jit(solution)/shard_map/pallas_call | solution.py:481
  106.3 0.0 copy-start
  106.3 2.4 %copy.14 = bf16[256,2048]{1,0:T(8,128)(2,1)} copy(bf16[256,2048]{1,0:T(8,128)(2,1)} %get-tuple-element.8) | data formatting | bytes 2097152
  108.7 0.0 copy-done
  108.7 0.0 copy-start.2
  108.7 1.0 copy.15
  109.7 0.1 copy-done.2
  109.7 0.0 copy-start.1
  109.7 0.7 copy.16
  110.4 0.3 copy-done.1
  110.7 0.7 copy.17
Async XLA Ops:
  106.3 2.4 %copy-start = (bf16[256,2048]{1,0:T(8,128)(2,1)S(1)}, bf16[256,2048]{1,0:T(8,128)(2,1)}, u32[]{:S(2)}) copy-start(bf16[256,2048]{1,0:T(8,128)(2,1)} %get-tuple-element.9) | copy-start | bytes 3145732
  108.7 1.0 copy-start.2
  109.7 1.0 copy-start.1

commit v5 on v4

--- a/solution.py
+++ b/solution.py
@@ -35,8 +35,8 @@
     do_ref,
     k_ref,
     v_ref,
-    out_ref,
-    dq_ref,
+    recv,
+    tab_v,
     dk_ref,
     dv_ref,
     kv,
@@ -58,10 +58,9 @@
     g_rsem,
     a_ssem,
     a_rsem,
-    tab_v,
     tab_s,
     tab_sem,
-    *recv,
+    own_sem,
 ):
     me = lax.axis_index("ctx")
     tok, width = q_ref.shape
@@ -378,17 +377,25 @@
             dq_t = dot_nn(kt[g], ds_scr[j]) * scale
             blocks[1, :, :, j * D : (j + 1) * D] = dq_t.T.astype(BF16).reshape(bpd, BLK, D)
 
+    def lanes(ch):
+        return pl.ds(pl.multiple_of(ch * CHUNK * D, CHUNK * D), CHUNK * D)
+
     def block_copy(ch, o):
         target = lax.rem(me + o, n)
         return pltpu.make_async_remote_copy(
             src_ref=send.at[ch, target],
-            dst_ref=recv[ch].at[me],
+            dst_ref=recv.at[me, :, :, :, lanes(ch)],
             send_sem=a_ssem.at[ch],
             recv_sem=a_rsem.at[ch],
             device_id={"ctx": target},
             device_id_type=pl.DeviceIdType.MESH,
         )
 
+    def own_copy(ch):
+        return pltpu.make_async_copy(
+            send.at[ch, me], recv.at[me, :, :, :, lanes(ch)], own_sem.at[ch]
+        )
+
     def chunk_step(ch, carry):
         g = ch // chunks_group
         first = lax.rem(ch, chunks_group) == 0
@@ -412,13 +419,9 @@
                 b = tab_s[0, t * CAP + c]
                 send[ch, t, c, 0] = blocks[0, b]
                 send[ch, t, c, 1] = blocks[1, b]
-        for cc in range(chunks):
-
-            @pl.when(ch == cc)
-            def _(cc=cc):
-                recv[cc][me] = send[cc, me]
-                for o in range(1, n):
-                    block_copy(cc, o).start()
+        for o in range(1, n):
+            block_copy(ch, o).start()
+        own_copy(ch).start()
 
         for g2 in range(1, groups):
 
@@ -439,32 +442,46 @@
         return carry
 
     lax.fori_loop(0, chunks, chunk_step, 0)
-
-    def unpack(ch):
-        held = recv[ch].at[pl.ds(0, n - 1)]
-        pltpu.make_async_copy(held, held, a_rsem.at[ch]).wait()
-        for slot in range(bpd):
-            w = tab_s[1, slot]
-            rows = slice(slot * BLK, (slot + 1) * BLK)
-            cols = slice(ch * CHUNK * D, (ch + 1) * CHUNK * D)
-            out_ref[rows, cols] = recv[ch][w // CAP, w % CAP, 0]
-            dq_ref[rows, cols] = recv[ch][w // CAP, w % CAP, 1]
 
     reduce_two(groups - 1)
     reduce_three(groups - 1)
     for g in range(groups - 1):
         reduce_last(g)
     reduce_four(groups - 1)
+    reduce_last(groups - 1)
+
     for ch in range(chunks):
-        unpack(ch)
-    reduce_last(groups - 1)
-
-    for ch in range(chunks):
+        own_copy(ch).wait()
         sent = send.at[ch, pl.ds(0, n - 1)]
         pltpu.make_async_copy(sent, sent, a_ssem.at[ch]).wait()
+        held = recv.at[pl.ds(0, n - 1), :, :, :, lanes(ch)]
+        pltpu.make_async_copy(held, held, a_rsem.at[ch]).wait()
     for g in range(groups):
         stage_sent(g)
         reduce_sent(g)
+
+
+def place_kernel(
+    tab_ref, recv, dk_in, dv_in, out_ref, dq_ref, dk_ref, dv_ref, held, kept, in_sem, out_sem
+):
+    bpd = out_ref.shape[0] // BLK
+    moves = []
+    for slot in range(bpd):
+        w = tab_ref[1, slot]
+        rows = pl.ds(slot * BLK, BLK)
+        for i, ref in enumerate((out_ref, dq_ref)):
+            moves.append((recv.at[w // CAP, w % CAP, i], held.at[i, slot], ref.at[rows]))
+    for i, (source, ref) in enumerate(((dk_in, dk_ref), (dv_in, dv_ref))):
+        moves.append((source, kept.at[i], ref))
+    loads = [pltpu.make_async_copy(m[0], m[1], in_sem.at[i]) for i, m in enumerate(moves)]
+    stores = [pltpu.make_async_copy(m[1], m[2], out_sem.at[i]) for i, m in enumerate(moves)]
+    for load in loads:
+        load.start()
+    for load, store in zip(loads, stores):
+        load.wait()
+        store.start()
+    for store in stores:
+        store.wait()
 
 
 def shards(q, k, v, do, lens, dest):
@@ -478,16 +495,17 @@
     keys = pieces * tok
     smem = pl.BlockSpec(memory_space=pltpu.SMEM)
     vmem = pl.BlockSpec(memory_space=pltpu.VMEM)
-    return pl.pallas_call(
+    hbm = pl.BlockSpec(memory_space=pl.ANY)
+    recv, tab, dk, dv = pl.pallas_call(
         functools.partial(main_kernel, n, pieces),
         out_shape=(
-            jax.ShapeDtypeStruct(q.shape, BF16),
-            jax.ShapeDtypeStruct(q.shape, BF16),
+            jax.ShapeDtypeStruct((n, CAP, 2, BLK, width), BF16),
+            jax.ShapeDtypeStruct((2, n * bpd), jnp.int32),
             jax.ShapeDtypeStruct(k.shape, BF16),
             jax.ShapeDtypeStruct(v.shape, BF16),
         ),
         in_specs=[smem, vmem, vmem, vmem, vmem, vmem],
-        out_specs=(vmem, vmem, vmem, vmem),
+        out_specs=(hbm, vmem, vmem, vmem),
         scratch_shapes=[
             pltpu.VMEM((4 * ROW - 1, groups, 2, tok, D), BF16),
             pltpu.VMEM((groups, D, keys), BF16),
@@ -508,15 +526,31 @@
             pltpu.SemaphoreType.DMA((3 * ROW, groups)),
             pltpu.SemaphoreType.DMA((chunks,)),
             pltpu.SemaphoreType.DMA((chunks,)),
-            pltpu.VMEM((2, n * bpd), jnp.int32),
             pltpu.SMEM((2, n * bpd), jnp.int32),
             pltpu.SemaphoreType.DMA(()),
-        ]
-        + [pltpu.VMEM((n, CAP, 2, BLK, CHUNK * D), BF16)] * chunks,
+            pltpu.SemaphoreType.DMA((chunks,)),
+        ],
         compiler_params=pltpu.CompilerParams(
             collective_id=0, has_side_effects=True, vmem_limit_bytes=60 * 2**20
         ),
     )(lens, dest.reshape(1, n * bpd), q, do, k, v)
+    return pl.pallas_call(
+        place_kernel,
+        out_shape=(
+            jax.ShapeDtypeStruct(q.shape, BF16),
+            jax.ShapeDtypeStruct(q.shape, BF16),
+            jax.ShapeDtypeStruct(k.shape, BF16),
+            jax.ShapeDtypeStruct(v.shape, BF16),
+        ),
+        in_specs=[smem, hbm, hbm, hbm],
+        out_specs=(hbm, hbm, hbm, hbm),
+        scratch_shapes=[
+            pltpu.VMEM((2, bpd, BLK, width), BF16),
+            pltpu.VMEM((2, *k.shape), BF16),
+            pltpu.SemaphoreType.DMA((2 * bpd + 2,)),
+            pltpu.SemaphoreType.DMA((2 * bpd + 2,)),
+        ],
+    )(tab, recv, dk, dv)
 
 
 def solution(mesh):

time: 112 us -> 110 us (0.982)
  local copies, waits for them, and re-layouts: 5.02 us -> 0 us
  Pallas kernels: 106 us -> 109 us
    unnamed x10 -> x0, local copies, waits for them, and re-layouts: 5.02 us -> none
    pallas_call x0 -> x1, Pallas kernels: none -> 3.67 us  [shards(): pl.pallas_call(place_kernel, out_shape=(jax.ShapeDtypeStruct(q.shape, BF1...]
where the time goes in v5:
time: 110 us; the launch traced here: 109 us
  Pallas kernels  109 us (99%)
    pallas_call x1, Pallas kernels, shards(): pl.pallas_call(functools.partial(main_kernel, n, pieces), out_shape=(jax....  105 us
    pallas_call x1, Pallas kernels, shards(): pl.pallas_call(place_kernel, out_shape=(jax.ShapeDtypeStruct(q.shape, BF1...  3.67 us

profile of v5, /device:TPU:66, one launch (start us, length us, event | category | flops | bytes accessed | tf_op | source)
XLA Modules:
  0.0 109.2 jit_solution(4913488172571342348)
XLA Ops:
  0.6 104.9 %shard_map.93 = (bf16[16,2,2,16,2048]{4,3,2,1,0:T(8,128)(2,1)}, s32[2,256]{1,0:T(2,128)}, bf16[256,256]{1,0:T(8,128)(2,1)}, bf16[256,256]{1,0:T(8,128)(2,1)}) custom-call(s32[8]{0:T(128)} %lens_ref.1, s32[1,256]{1,0:T(1,128)} %bitcast.1, bf16[256,2048]{1,0:T(8,128)(2,1)} %q_ref.1, bf16[256,2048]{1,0:T(8,128)(2,1)} %do_ref.1, bf16[256,256]{1,0:T(8,128)(2,1)} %k_ref.1, ...), custom_call_target="tpu_custom_call" | custom-call | tf_op jit(solution)/shard_map/pallas_call | solution.py:499
  105.5 3.7 %shard_map.94 = (bf16[256,2048]{1,0:T(8,128)(2,1)}, bf16[256,2048]{1,0:T(8,128)(2,1)}, bf16[256,256]{1,0:T(8,128)(2,1)}, bf16[256,256]{1,0:T(8,128)(2,1)}) custom-call(s32[2,256]{1,0:T(2,128)} %get-tuple-element.8.tab_ref, bf16[16,2,2,16,2048]{4,3,2,1,0:T(8,128)(2,1)} %get-tuple-element.9.recv, bf16[256,256]{1,0:T(8,128)(2,1)} %get-tuple-element.10.dk_in, ...), custom_call_target="tpu_custom_call" | custom-call | tf_op jit(solution)/shard_map/pallas_call | solution.py:537

commit v6 on v5

--- a/solution.py
+++ b/solution.py
@@ -31,8 +31,8 @@
     pieces,
     lens_ref,
     dest_ref,
-    q_ref,
-    do_ref,
+    q_hbm,
+    do_hbm,
     k_ref,
     v_ref,
     recv,
@@ -61,9 +61,14 @@
     tab_s,
     tab_sem,
     own_sem,
+    q_ref,
+    do_ref,
+    in_sem,
 ):
     me = lax.axis_index("ctx")
     tok, width = q_ref.shape
+    q_load = pltpu.make_async_copy(q_hbm, q_ref, in_sem.at[0])
+    do_load = pltpu.make_async_copy(do_hbm, do_ref, in_sem.at[1])
     heads = width // D
     groups = k_ref.shape[1] // D
     per_group = heads // groups
@@ -89,12 +94,6 @@
     for g in range(groups):
         kv[base, g, 0] = k_ref[:, g * D : (g + 1) * D]
         kv[base, g, 1] = v_ref[:, g * D : (g + 1) * D]
-    for d in range(1, pieces):
-
-        @pl.when(me < d)
-        def _(d=d):
-            kv[base + d] = jnp.zeros_like(kv[base + d])
-
     pl.semaphore_wait(barrier, n - 1)
 
     def hop(g, message, src, dst, dx, ty, go):
@@ -132,7 +131,7 @@
 
     def stage_one(g):
         hop(g, 0, 0, ROW, 1, y, below)
-        for k in range(1, ROW):
+        for k in (1, 3, 2):
             hop(g, k, 0, beside(k) - y, 0, beside(k), row_go[k])
         hop(g, ROW, 0, 3 * ROW - y, 3, 0, third)
 
@@ -282,6 +281,14 @@
                 pltpu.make_async_copy(held, held, g_ssem.at[message, g]).wait()
 
     stage_one(0)
+    q_load.start()
+    do_load.start()
+
+    for d in range(1, pieces):
+
+        @pl.when(me < d)
+        def _(d=d):
+            kv[base + d] = jnp.zeros_like(kv[base + d])
 
     nb = n * bpd
     lane = lax.broadcasted_iota(jnp.int32, (nb, nb), 1)
@@ -316,6 +323,8 @@
     to_smem.wait()
     stage_two(0)
     stage_three(0)
+    q_load.wait()
+    do_load.wait()
     for g in range(1, groups):
         stage_one(g)
 
@@ -504,7 +513,7 @@
             jax.ShapeDtypeStruct(k.shape, BF16),
             jax.ShapeDtypeStruct(v.shape, BF16),
         ),
-        in_specs=[smem, vmem, vmem, vmem, vmem, vmem],
+        in_specs=[smem, vmem, hbm, hbm, vmem, vmem],
         out_specs=(hbm, vmem, vmem, vmem),
         scratch_shapes=[
             pltpu.VMEM((4 * ROW - 1, groups, 2, tok, D), BF16),
@@ -529,6 +538,9 @@
             pltpu.SMEM((2, n * bpd), jnp.int32),
             pltpu.SemaphoreType.DMA(()),
             pltpu.SemaphoreType.DMA((chunks,)),
+            pltpu.VMEM(q.shape, BF16),
+            pltpu.VMEM(q.shape, BF16),
+            pltpu.SemaphoreType.DMA((2,)),
         ],
         compiler_params=pltpu.CompilerParams(
             collective_id=0, has_side_effects=True, vmem_limit_bytes=60 * 2**20

time: 110 us -> 109 us (level)
  no operation moved by 1% of the time
where the time goes in v6:
time: 109 us
  Pallas kernels  108 us (99%)
    pallas_call x1, Pallas kernels, shards(): pl.pallas_call(functools.partial(main_kernel, n, pieces), out_shape=(jax....  104 us
    pallas_call x1, Pallas kernels, shards(): pl.pallas_call(place_kernel, out_shape=(jax.ShapeDtypeStruct(q.shape, BF1...  3.67 us

profile of v6, /device:TPU:66, one launch (start us, length us, event | category | flops | bytes accessed | tf_op | source)
XLA Modules:
  0.0 108.7 jit_solution(15543196961207843894)
XLA Ops:
  0.6 104.4 %shard_map.93 = (bf16[16,2,2,16,2048]{4,3,2,1,0:T(8,128)(2,1)}, s32[2,256]{1,0:T(2,128)}, bf16[256,256]{1,0:T(8,128)(2,1)}, bf16[256,256]{1,0:T(8,128)(2,1)}) custom-call(s32[8]{0:T(128)} %lens_ref.1, s32[1,256]{1,0:T(1,128)} %bitcast.1, bf16[256,2048]{1,0:T(8,128)(2,1)} %q_hbm.1, bf16[256,2048]{1,0:T(8,128)(2,1)} %do_hbm.1, bf16[256,256]{1,0:T(8,128)(2,1)} %k_ref.1, ...), custom_call_target="tpu_custom_call" | custom-call | tf_op jit(solution)/shard_map/pallas_call | solution.py:508
  105.1 3.7 %shard_map.94 = (bf16[256,2048]{1,0:T(8,128)(2,1)}, bf16[256,2048]{1,0:T(8,128)(2,1)}, bf16[256,256]{1,0:T(8,128)(2,1)}, bf16[256,256]{1,0:T(8,128)(2,1)}) custom-call(s32[2,256]{1,0:T(2,128)} %get-tuple-element.8.tab_ref, bf16[16,2,2,16,2048]{4,3,2,1,0:T(8,128)(2,1)} %get-tuple-element.9.recv, bf16[256,256]{1,0:T(8,128)(2,1)} %get-tuple-element.10.dk_in, ...), custom_call_target="tpu_custom_call" | custom-call | tf_op jit(solution)/shard_map/pallas_call | solution.py:549

commit v7 on v6

--- a/solution.py
+++ b/solution.py
@@ -221,9 +221,9 @@
     ]
 
     def reduce_one(g):
+        give(g, 4, 2 * ROW + y - opp, 1, y, gives[4])
         give(g, 0, 2 * ROW + y - nxt, 0, nxt, gives[0])
         give(g, 1, 2 * ROW + y - prv, 0, prv, gives[1])
-        give(g, 4, 2 * ROW + y - opp, 1, y, gives[4])
         give(g, 7, 2 * ROW + 1, 3, ROW - 1, gives[7])
         give(g, 2, ROW + y - nxt, 0, nxt, gives[2])
         give(g, 3, ROW + y - prv, 0, prv, gives[3])
@@ -234,10 +234,10 @@
         take(g, 0, 2 * ROW, (x >= 2) & (2 * ROW + prv - y < pieces))
         take(g, 1, 2 * ROW, (x >= 2) & (2 * ROW + nxt - y < pieces))
         give(g, 8, 2 * ROW, 1, y, gives[8])
-
-    def reduce_three(g):
         take(g, 4, ROW + y - opp, (x >= 1) & below & (2 * ROW + y - opp < pieces))
         give(g, 10, ROW + y - opp, 1, y, gives[10])
+
+    def reduce_three(g):
         take(g, 2, ROW, x >= 1)
         take(g, 3, ROW, x >= 1)
         take(g, 8, ROW, (x >= 1) & below)
@@ -428,9 +428,19 @@
                 b = tab_s[0, t * CAP + c]
                 send[ch, t, c, 0] = blocks[0, b]
                 send[ch, t, c, 1] = blocks[1, b]
-        for o in range(1, n):
-            block_copy(ch, o).start()
-        own_copy(ch).start()
+        held_back = chunks - 2
+
+        @pl.when(ch == held_back + 1)
+        def _():
+            for o in range(1, n):
+                block_copy(ch - 1, o).start()
+            own_copy(ch - 1).start()
+
+        @pl.when(ch != held_back)
+        def _():
+            for o in range(1, n):
+                block_copy(ch, o).start()
+            own_copy(ch).start()
 
         for g2 in range(1, groups):
 
@@ -474,23 +484,31 @@
     tab_ref, recv, dk_in, dv_in, out_ref, dq_ref, dk_ref, dv_ref, held, kept, in_sem, out_sem
 ):
     bpd = out_ref.shape[0] // BLK
-    moves = []
+    loads, stores = [], []
     for slot in range(bpd):
         w = tab_ref[1, slot]
         rows = pl.ds(slot * BLK, BLK)
-        for i, ref in enumerate((out_ref, dq_ref)):
-            moves.append((recv.at[w // CAP, w % CAP, i], held.at[i, slot], ref.at[rows]))
+        loads.append(
+            pltpu.make_async_copy(recv.at[w // CAP, w % CAP], held.at[slot], in_sem.at[slot])
+        )
+        stores.append(
+            [
+                pltpu.make_async_copy(held.at[slot, i], ref.at[rows], out_sem.at[2 * slot + i])
+                for i, ref in enumerate((out_ref, dq_ref))
+            ]
+        )
     for i, (source, ref) in enumerate(((dk_in, dk_ref), (dv_in, dv_ref))):
-        moves.append((source, kept.at[i], ref))
-    loads = [pltpu.make_async_copy(m[0], m[1], in_sem.at[i]) for i, m in enumerate(moves)]
-    stores = [pltpu.make_async_copy(m[1], m[2], out_sem.at[i]) for i, m in enumerate(moves)]
+        loads.append(pltpu.make_async_copy(source, kept.at[i], in_sem.at[bpd + i]))
+        stores.append([pltpu.make_async_copy(kept.at[i], ref, out_sem.at[2 * bpd + i])])
     for load in loads:
         load.start()
-    for load, store in zip(loads, stores):
+    for load, group in zip(loads, stores):
         load.wait()
-        store.start()
-    for store in stores:
-        store.wait()
+        for store in group:
+            store.start()
+    for group in stores:
+        for store in group:
+            store.wait()
 
 
 def shards(q, k, v, do, lens, dest):
@@ -557,9 +575,9 @@
         in_specs=[smem, hbm, hbm, hbm],
         out_specs=(hbm, hbm, hbm, hbm),
         scratch_shapes=[
-            pltpu.VMEM((2, bpd, BLK, width), BF16),
+            pltpu.VMEM((bpd, 2, BLK, width), BF16),
             pltpu.VMEM((2, *k.shape), BF16),
-            pltpu.SemaphoreType.DMA((2 * bpd + 2,)),
+            pltpu.SemaphoreType.DMA((bpd + 2,)),
             pltpu.SemaphoreType.DMA((2 * bpd + 2,)),
         ],
     )(tab, recv, dk, dv)

time: 109 us -> 109 us (level)
  no operation moved by 1% of the time
where the time goes in v7:
time: 109 us; the launch traced here: 108 us
  Pallas kernels  107 us (98%)
    pallas_call x1, Pallas kernels, shards(): pl.pallas_call(functools.partial(main_kernel, n, pieces), out_shape=(jax....  104 us
    pallas_call x1, Pallas kernels, shards(): pl.pallas_call(place_kernel, out_shape=(jax.ShapeDtypeStruct(q.shape, BF1...  3.53 us

profile of v7, /device:TPU:66, one launch (start us, length us, event | category | flops | bytes accessed | tf_op | source)
XLA Modules:
  0.0 107.8 jit_solution(17907480243792868016)
XLA Ops:
  0.6 103.6 %shard_map.93 = (bf16[16,2,2,16,2048]{4,3,2,1,0:T(8,128)(2,1)}, s32[2,256]{1,0:T(2,128)}, bf16[256,256]{1,0:T(8,128)(2,1)}, bf16[256,256]{1,0:T(8,128)(2,1)}) custom-call(s32[8]{0:T(128)} %lens_ref.1, s32[1,256]{1,0:T(1,128)} %bitcast.1, bf16[256,2048]{1,0:T(8,128)(2,1)} %q_hbm.1, bf16[256,2048]{1,0:T(8,128)(2,1)} %do_hbm.1, bf16[256,256]{1,0:T(8,128)(2,1)} %k_ref.1, ...), custom_call_target="tpu_custom_call" | custom-call | tf_op jit(solution)/shard_map/pallas_call | solution.py:526
  104.3 3.5 %shard_map.94 = (bf16[256,2048]{1,0:T(8,128)(2,1)}, bf16[256,2048]{1,0:T(8,128)(2,1)}, bf16[256,256]{1,0:T(8,128)(2,1)}, bf16[256,256]{1,0:T(8,128)(2,1)}) custom-call(s32[2,256]{1,0:T(2,128)} %get-tuple-element.8.tab_ref, bf16[16,2,2,16,2048]{4,3,2,1,0:T(8,128)(2,1)} %get-tuple-element.9.recv, bf16[256,256]{1,0:T(8,128)(2,1)} %get-tuple-element.10.dk_in, ...), custom_call_target="tpu_custom_call" | custom-call | tf_op jit(solution)/shard_map/pallas_call | solution.py:567
